TPU v7x, 512 devices: a whole 4x8x8 slice. The times are simulated.
512 devices in a mesh: dp: 64 (over y, z_hi, core), tensor: 8 (over x, z_lo).
Axes of the slice: x: 4, y: 8, z: 8 (z_hi: 4, z_lo: 2; z = z_hi * 2 + z_lo), core: 2. Of those that a mesh axis runs over, the one named last changes fastest.
Arguments:
- inputs: float32 [16384, 1024], P('dp', 'tensor'), may hold values from -16 to 16
- cotangent: float32 [16384, 1024], P('dp', 'tensor'), may hold values from -0.12 to 0.12
- gate_weight: float32 [1024, 4096], P('dp', 'tensor'), may hold values from -0.1875 to 0.1875
- up_weight: float32 [1024, 4096], P('dp', 'tensor'), may hold values from -0.1875 to 0.1875
- down_weight: float32 [1024, 4096], P('dp', 'tensor'), may hold values from -0.09375 to 0.09375
- gate_first: float32 [1024, 4096], P('dp', 'tensor'), may hold values from -6 to 6
- gate_second: float32 [1024, 4096], P('dp', 'tensor'), may hold values from 0.5 to 4
- up_first: float32 [1024, 4096], P('dp', 'tensor'), may hold values from -6 to 6
- up_second: float32 [1024, 4096], P('dp', 'tensor'), may hold values from 0.5 to 4
Outputs:
- gate_new: float32 [1024, 4096], P('dp', 'tensor')
- gate_first_new: float32 [1024, 4096], P('dp', 'tensor')
- gate_second_new: float32 [1024, 4096], P('dp', 'tensor')
- up_new: float32 [1024, 4096], P('dp', 'tensor')
- up_first_new: float32 [1024, 4096], P('dp', 'tensor')
- up_second_new: float32 [1024, 4096], P('dp', 'tensor')
All inputs are finite; a program needn't handle non-finite values.
Results may differ from a plain program's by a relative error of at most 0.00005.
Values sent between devices are 32-bit elements; how exact they have to be, the bound alone decides.
A program may use at most 64 MiB of HBM per device.

v0:
```python
import jax
import jax.numpy as jnp
from jax import lax
from jax.sharding import PartitionSpec as P

STEP = 100


def adam_update(weight, first, second, grad):
    first_new = 0.9 * first + 0.1 * grad
    second_new = 0.95 * second + 0.05 * grad * grad
    first_hat = first_new / (1.0 - 0.9**STEP)
    second_hat = second_new / (1.0 - 0.95**STEP)
    weight_new = weight - 0.003 * first_hat / (jnp.sqrt(second_hat) + 1e-08)
    return (weight_new, first_new, second_new)


def contract(left, piece):
    return jnp.dot(left, piece, precision=lax.Precision.HIGHEST, preferred_element_type=jnp.float32)


def local(
    inputs,
    cotangent,
    gate_weight,
    up_weight,
    down_weight,
    gate_first,
    gate_second,
    up_first,
    up_second,
):
    rows_full, cot_full = (
        lax.all_gather(inputs, "tensor", axis=1, tiled=True),
        lax.all_gather(cotangent, "tensor", axis=1, tiled=True),
    )
    gate_sum = contract(rows_full, lax.all_gather(gate_weight, "dp", axis=0, tiled=True))
    lift_sum = contract(rows_full, lax.all_gather(up_weight, "dp", axis=0, tiled=True))
    back_sum = contract(cot_full, lax.all_gather(down_weight, "dp", axis=0, tiled=True))
    sigmoid_gate = jax.nn.sigmoid(gate_sum)
    gate_rows = back_sum * lift_sum * sigmoid_gate * (1.0 + gate_sum * (1.0 - sigmoid_gate))
    lift_rows = back_sum * gate_sum * sigmoid_gate

    def make_term(grad_rows):
        return lax.dot_general(
            rows_full,
            grad_rows,
            (((0,), (0,)), ((), ())),
            precision=lax.Precision.HIGHEST,
            preferred_element_type=jnp.float32,
        )

    gate_grad = lax.psum_scatter(make_term(gate_rows), "dp", scatter_dimension=0, tiled=True)
    lift_grad = lax.psum_scatter(make_term(lift_rows), "dp", scatter_dimension=0, tiled=True)
    gate_new, gate_first_new, gate_second_new = adam_update(
        gate_weight, gate_first, gate_second, gate_grad
    )
    up_new, up_first_new, up_second_new = adam_update(up_weight, up_first, up_second, lift_grad)
    return (gate_new, gate_first_new, gate_second_new, up_new, up_first_new, up_second_new)


def solution(mesh):
    in_specs = (
        P("dp", "tensor"),
        P("dp", "tensor"),
        P("dp", "tensor"),
        P("dp", "tensor"),
        P("dp", "tensor"),
        P("dp", "tensor"),
        P("dp", "tensor"),
        P("dp", "tensor"),
        P("dp", "tensor"),
    )
    out_specs = (
        P("dp", "tensor"),
        P("dp", "tensor"),
        P("dp", "tensor"),
        P("dp", "tensor"),
        P("dp", "tensor"),
        P("dp", "tensor"),
    )
    return jax.shard_map(local, mesh=mesh, in_specs=in_specs, out_specs=out_specs, check_vma=False)
```

profile of v0, /device:TPU:1, one launch (start us, length us, event | category | flops | bytes accessed | tf_op | source)
XLA Modules:
  0.0 679.3 jit_solution(2127603420906008118)
XLA Ops:
  7.2 0.0 all-gather.6.cloned.1.call-start
  7.2 0.7 all-gather.6.cloned.1.call-update
  7.9 0.0 all-gather.8.cloned.1.call-start
  7.9 0.7 all-gather.8.cloned.1.call-update
  8.6 0.0 all-gather.10.cloned.1.call-start
  8.7 0.7 all-gather.10.cloned.1.call-update
  9.4 0.0 all-gather.14.cloned.1.call-start
  9.4 0.5 all-gather.14.cloned.1.call-update
  10.0 0.0 all-gather.12.cloned.1.call-start
  10.0 0.5 all-gather.12.cloned.1.call-update
  10.5 0.0 reduce-scatter.9.cloned.1.call-start
  10.6 45.9 %all-gather.6.cloned.1.call-done = f32[256,1024]{1,0:T(8,128)} async-done(((f32[256,128]{1,0:T(8,128)}), f32[256,1024]{1,0:T(8,128)}) %all-gather.6.cloned.1.call-update) | async-done | bytes 1048592 | tf_op jit(solution)/shard_map/all_gather | solution.py:35
  56.5 94.2 %all-gather.8.cloned.1.call-done = f32[1024,512]{1,0:T(8,128)} async-done(((f32[16,512]{1,0:T(8,128)}), f32[1024,512]{1,0:T(8,128)}) %all-gather.8.cloned.1.call-update) | async-done | bytes 2097168 | tf_op jit(solution)/shard_map/all_gather | solution.py:39
  150.6 4.7 fusion.10
  155.4 34.7 %all-gather.10.cloned.1.call-done = f32[256,1024]{1,0:T(8,128)} async-done(((f32[256,128]{1,0:T(8,128)}), f32[256,1024]{1,0:T(8,128)}) %all-gather.10.cloned.1.call-update) | async-done | bytes 1048592 | tf_op jit(solution)/shard_map/all_gather | solution.py:34
  190.0 0.0 copy-start
  190.0 94.0 %all-gather.14.cloned.1.call-done = f32[1024,512]{1,0:T(8,128)} async-done(((f32[16,512]{1,0:T(8,128)}), f32[1024,512]{1,0:T(8,128)}) %all-gather.14.cloned.1.call-update) | async-done | bytes 2097168 | tf_op jit(solution)/shard_map/all_gather | solution.py:37
  284.1 0.0 copy-start.1
  284.1 3.9 fusion.11
  288.0 0.0 copy-start.3
  288.0 0.8 copy-done.3
  288.8 0.0 copy-done
  288.8 0.0 copy-done.1
  288.8 2.0 convolution_bitcast_fusion
  290.8 1.8 copy.55
  292.6 0.0 copy-start.2
  292.6 0.0 copy-start.4
  292.6 0.0 reduce-scatter.9.cloned.1.call-update
  292.6 0.0 reduce-scatter.7.cloned.1.call-start
  292.6 76.3 %all-gather.12.cloned.1.call-done = f32[1024,512]{1,0:T(8,128)} async-done(((f32[16,512]{1,0:T(8,128)}), f32[1024,512]{1,0:T(8,128)}) %all-gather.12.cloned.1.call-update) | async-done | bytes 2097168 | tf_op jit(solution)/shard_map/all_gather | solution.py:38
  368.9 0.0 copy-done.2
  369.0 0.0 copy-done.4
  369.0 3.6 fusion.1
  372.6 1.9 convolution_bitcast_fusion.1
  374.5 1.8 copy.53
  376.3 0.0 copy-start.5
  376.3 0.0 copy-start.7
  376.3 0.0 copy-start.8
  376.3 0.0 copy-start.6
  376.3 0.0 copy-start.9
  376.3 0.0 copy-start.10
  376.3 0.0 reduce-scatter.7.cloned.1.call-update
  376.4 141.1 %reduce-scatter.9.cloned.1.call-done = f32[16,512]{1,0:T(8,128)} async-done(((f32[1024,512]{1,0:T(8,128)}), f32[16,512]{1,0:T(8,128)}) %reduce-scatter.9.cloned.1.call-update) | async-done | bytes 32784 | tf_op jit(solution)/shard_map/reduce_scatter | solution.py:54
  517.5 0.0 copy-done.5
  517.5 0.0 copy-done.7
  517.5 0.0 copy-done.8
  517.5 1.4 divide_subtract_fusion
  518.9 152.1 %reduce-scatter.7.cloned.1.call-done = f32[16,512]{1,0:T(8,128)} async-done(((f32[1024,512]{1,0:T(8,128)}), f32[16,512]{1,0:T(8,128)}) %reduce-scatter.7.cloned.1.call-update) | async-done | bytes 32784 | tf_op jit(solution)/shard_map/reduce_scatter | solution.py:53
  671.0 0.0 copy-done.6
  671.0 0.0 copy-done.9
  671.0 0.0 copy-done.10
  671.0 1.4 divide_subtract_fusion.1
Async XLA Ops:
  7.2 49.3 %all-gather.6.cloned.1.call-start = ((), (), s32[]{:S(2)}) async-start(), calls=%async_computation.2 | async-start | bytes 1179648 | tf_op jit(solution)/shard_map/all_gather | solution.py:35
  7.9 142.7 %all-gather.8.cloned.1.call-start = ((), (), s32[]{:S(2)}) async-start(), calls=%async_computation.3 | async-start | bytes 2129920 | tf_op jit(solution)/shard_map/all_gather | solution.py:39
  8.6 181.4 %all-gather.10.cloned.1.call-start = ((), (), s32[]{:S(2)}) async-start(), calls=%async_computation.4 | async-start | bytes 1179648 | tf_op jit(solution)/shard_map/all_gather | solution.py:34
  9.4 274.7 %all-gather.14.cloned.1.call-start = ((), (), s32[]{:S(2)}) async-start(), calls=%async_computation.6 | async-start | bytes 2129920 | tf_op jit(solution)/shard_map/all_gather | solution.py:37
  10.0 359.0 %all-gather.12.cloned.1.call-start = ((), (), s32[]{:S(2)}) async-start(), calls=%async_computation.5 | async-start | bytes 2129920 | tf_op jit(solution)/shard_map/all_gather | solution.py:38
  10.5 507.0 %reduce-scatter.9.cloned.1.call-start = ((), (), s32[]{:S(2)}) async-start(), calls=%async_computation.8 | async-start | bytes 2129920 | tf_op jit(solution)/shard_map/reduce_scatter | solution.py:54
  190.0 98.7 %copy-start = (f32[256,1024]{1,0:T(8,128)S(1)}, f32[256,1024]{1,0:T(8,128)}, u32[]{:S(2)}) copy-start(f32[256,1024]{1,0:T(8,128)} %all-gather.10.cloned.1.call-done) | copy-start | bytes 3145732
  284.1 4.7 copy-start.1
  288.0 0.8 copy-start.3
  292.6 76.4 %copy-start.2 = (f32[256,512]{1,0:T(8,128)S(1)}, f32[256,512]{1,0:T(8,128)}, u32[]{:S(2)}) copy-start(f32[256,512]{1,0:T(8,128)} %fusion.10) | copy-start | bytes 1572868
  292.6 76.4 %copy-start.4 = (f32[256,512]{1,0:T(8,128)S(1)}, f32[256,512]{1,0:T(8,128)}, u32[]{:S(2)}) copy-start(f32[256,512]{1,0:T(8,128)} %copy-done.3) | copy-start | bytes 1572868
  292.6 378.4 %reduce-scatter.7.cloned.1.call-start = ((), (), s32[]{:S(2)}) async-start(), calls=%async_computation.7 | async-start | bytes 2129920 | tf_op jit(solution)/shard_map/reduce_scatter | solution.py:53
  376.3 141.2 %copy-start.5 = (f32[16,512]{1,0:T(8,128)S(1)}, f32[16,512]{1,0:T(8,128)}, u32[]{:S(2)}) copy-start(f32[16,512]{1,0:T(8,128)} %param.12) | copy-start | bytes 98308
  376.3 141.2 %copy-start.7 = (f32[16,512]{1,0:T(8,128)S(1)}, f32[16,512]{1,0:T(8,128)}, u32[]{:S(2)}) copy-start(f32[16,512]{1,0:T(8,128)} %param.16) | copy-start | bytes 98308
  376.3 141.2 %copy-start.8 = (f32[16,512]{1,0:T(8,128)S(1)}, f32[16,512]{1,0:T(8,128)}, u32[]{:S(2)}) copy-start(f32[16,512]{1,0:T(8,128)} %param.17) | copy-start | bytes 98308
  376.3 294.7 %copy-start.6 = (f32[16,512]{1,0:T(8,128)S(1)}, f32[16,512]{1,0:T(8,128)}, u32[]{:S(2)}) copy-start(f32[16,512]{1,0:T(8,128)} %param.11) | copy-start | bytes 98308
  376.3 294.7 %copy-start.9 = (f32[16,512]{1,0:T(8,128)S(1)}, f32[16,512]{1,0:T(8,128)}, u32[]{:S(2)}) copy-start(f32[16,512]{1,0:T(8,128)} %param.14) | copy-start | bytes 98308
  376.3 294.7 %copy-start.10 = (f32[16,512]{1,0:T(8,128)S(1)}, f32[16,512]{1,0:T(8,128)}, u32[]{:S(2)}) copy-start(f32[16,512]{1,0:T(8,128)} %param.15) | copy-start | bytes 98308
Sparse Core Ops, SparseCore 0:
  10.0 46.4 all-gather.5
  59.8 90.8 all-gather.7
  152.7 37.3 all-gather.9
  193.2 90.8 all-gather.13
  287.2 81.6 all-gather.11
  373.4 144.0 reduce-scatter.8
  522.1 148.8 reduce-scatter.6
where the time goes:
time: 683 us; the launch traced here: 679 us
  waiting for transfers between devices  641 us (94%)
  matrix products  16.1 us (2%)
  between operations  14.2 us (2%)
    reduce_scatter x1, waiting for transfers between devices, local(): lax.psum_scatter(make_term(gate_rows), 'dp', scatter_dimension=0, tiled=T...  152 us
    reduce_scatter x1, waiting for transfers between devices, local(): lax.psum_scatter(make_term(lift_rows), 'dp', scatter_dimension=0, tiled=T...  141 us
    all_gather x1, waiting for transfers between devices, local(): lax.all_gather(down_weight, 'dp', axis=0, tiled=True)  94.2 us
    all_gather x1, waiting for transfers between devices, local(): lax.all_gather(gate_weight, 'dp', axis=0, tiled=True)  94 us
    all_gather x1, waiting for transfers between devices, local(): lax.all_gather(up_weight, 'dp', axis=0, tiled=True)  76.3 us
    all_gather x1, waiting for transfers between devices, local(): lax.all_gather(cotangent, 'tensor', axis=1, tiled=True)  45.9 us
    all_gather x1, waiting for transfers between devices, local(): lax.all_gather(inputs, 'tensor', axis=1, tiled=True)  34.7 us
  transfers between devices with their start and end apart: 7, of which 7 were waited for; matrix products, arithmetic and copies ran while one was open for 3% of the time, Pallas kernels for 0%

commit v1 on v0

v1 whole, which is shorter than its diff:
```python
import jax
import jax.numpy as jnp
from jax import lax
from jax.experimental import pallas as pl
from jax.experimental.pallas import tpu as pltpu
from jax.sharding import PartitionSpec as P

STEP = 100
MESH = pl.DeviceIdType.MESH
F32 = jnp.float32
BF16 = jnp.bfloat16
NX, NZL, NY, NZH = 4, 2, 8, 4


def adam_update(weight, first, second, grad):
    first_new = 0.9 * first + 0.1 * grad
    second_new = 0.95 * second + 0.05 * grad * grad
    first_hat = first_new / (1.0 - 0.9**STEP)
    second_hat = second_new / (1.0 - 0.95**STEP)
    weight_new = weight - 0.003 * first_hat / (jnp.sqrt(second_hat) + 1e-08)
    return (weight_new, first_new, second_new)


def split(v):
    hi = v.astype(BF16)
    return hi, (v - hi.astype(F32)).astype(BF16)


def dot(a, b):
    return jnp.dot(a, b, preferred_element_type=F32)


def dot3(ah, al, bh, bl):
    return dot(ah, bh) + dot(ah, bl) + dot(al, bh)


def kernel(
    in_ref, cot_ref, gw_ref, uw_ref, dw_ref, out_ref,
    xc, w, xh, xl, ch, cl, xth, xtl, wh, wl, acc, rh, rl, gbuf, rbuf, tbuf, zbuf,
    own_sem, a_recv, a_send, s_recv, s_send, w_recv, w_send, y_recv, y_send,
    r_recv, r_send, z_recv, z_send,
):
    dp = lax.axis_index("dp")
    t = lax.axis_index("tensor")
    c = lax.rem(dp, 2)
    zh = lax.rem(dp // 2, NZH)
    y = dp // (2 * NZH)
    x = t // NZL
    zl = lax.rem(t, NZL)

    def t_of(dx, dz):
        zz = zl if dz == 0 else 1 - zl
        return lax.rem(x + dx, NX) * NZL + zz

    def y_of(d):
        return lax.rem(y + d, NY)

    def dp_of(yy, zz, cc):
        return (yy * NZH + zz) * 2 + cc

    sib = (dp_of(y, zh, 1 - c), t)
    zpart = (dp, t_of(0, 1))
    xr = (dp, t_of(1, 0))
    xleft = (dp, t_of(3, 0))
    yr = (dp_of(y_of(1), zh, c), t)
    yl = (dp_of(y_of(7), zh, c), t)

    def zc_of(dz, dc):
        zz = lax.rem(zh + dz, NZH)
        cc = c if dc == 0 else 1 - c
        return zz, cc, (dp_of(y, zz, cc), t)

    zpeers = [(dz, dc) for dz in range(NZH) for dc in range(2) if (dz, dc) != (0, 0)]

    barrier = pltpu.get_barrier_semaphore()
    peers = [zc_of(dz, dc)[2] for dz, dc in zpeers] + [zpart, xr, xleft, yr, yl]
    for peer in peers:
        pl.semaphore_signal(barrier, inc=1, device_id=peer, device_id_type=MESH)
    pl.semaphore_wait(barrier, len(peers))

    def remote(src, dst, send, recv, dev):
        pltpu.make_async_remote_copy(
            src_ref=src, dst_ref=dst, send_sem=send, recv_sem=recv,
            device_id=dev, device_id_type=MESH,
        ).start()

    def wait(ref, sem):
        pltpu.make_async_copy(ref, ref, sem).wait()

    w_srcs = (dw_ref, gw_ref, uw_ref)

    def w_first(k):
        row = pl.multiple_of(zh * 32 + c * 16, 16)
        for dz, dc in [(1, 0), (1, 1), (3, 0), (3, 1), (2, 0), (2, 1), (0, 1)]:
            _, cc, dev = zc_of(dz, dc)
            col = pl.multiple_of(cc * 256, 256)
            remote(
                w_srcs[k].at[:, pl.ds(col, 256)],
                w.at[y, k, pl.ds(row, 16), :],
                w_send.at[k], w_recv.at[k], dev,
            )
        col = pl.multiple_of(c * 256, 256)
        pltpu.make_async_copy(
            w_srcs[k].at[:, pl.ds(col, 256)],
            w.at[y, k, pl.ds(row, 16), :],
            w_recv.at[k],
        ).start()

    own = t_of(0, 0)

    def own_rows(n, dev, send, recv):
        for j, src in enumerate((in_ref, cot_ref)):
            remote(src, xc.at[own, c, j], send.at[n], recv, dev)

    w_first(0)
    own_rows(0, xr, a_send, a_recv.at[3, 0])
    own_rows(1, xleft, a_send, a_recv.at[1, 0])
    own_rows(2, zpart, a_send, a_recv.at[0, 1])
    w_first(1)
    w_first(2)
    own_rows(3, sib, a_send, s_recv.at[0, 0])
    for j, src in enumerate((in_ref, cot_ref)):
        pltpu.make_async_copy(src, xc.at[own, c, j], own_sem).start()

    def y_send_step(s, k):
        if s < 4:
            b = y_of((9 - s) % 8)
            remote(w.at[b, k], w.at[b, k], y_send.at[0, s - 1, k], y_recv.at[0, s - 1, k], yr)
            b = y_of(s - 1)
            remote(w.at[b, k], w.at[b, k], y_send.at[1, s - 1, k], y_recv.at[1, s - 1, k], yl)
        else:
            b = y_of(5)
            r = w.at[b, k, pl.ds(0, 64), :]
            remote(r, r, y_send.at[0, 3, k], y_recv.at[0, 3, k], yr)
            b = y_of(3)
            r = w.at[b, k, pl.ds(64, 64), :]
            remote(r, r, y_send.at[1, 3, k], y_recv.at[1, 3, k], yl)

    def y_wait_step(s, k):
        if s < 4:
            wait(w.at[y_of(8 - s), k], y_recv.at[0, s - 1, k])
            wait(w.at[y_of(s), k], y_recv.at[1, s - 1, k])
        else:
            b = y_of(4)
            wait(w.at[b, k, pl.ds(0, 64), :], y_recv.at[0, 3, k])
            wait(w.at[b, k, pl.ds(64, 64), :], y_recv.at[1, 3, k])

    def to_sibling(dx, dz):
        b = xc.at[t_of(dx, dz), c]
        remote(b, b, s_send.at[dx, dz], s_recv.at[dx, dz], sib)

    def a_wait(dx, dz):
        wait(xc.at[t_of(dx, dz), c], a_recv.at[dx, dz])

    def from_right(dz):
        a_wait(1, dz)
        b = xc.at[t_of(1, dz), c, 1]
        remote(b, b, a_send.at[6 + dz], a_recv.at[2, dz], xleft)
        to_sibling(1, dz)

    def from_left(dz):
        a_wait(3, dz)
        b = xc.at[t_of(3, dz), c, 0]
        remote(b, b, a_send.at[8 + dz], a_recv.at[2, dz], xr)
        to_sibling(3, dz)

    def s_wait(dx, dz):
        wait(xc.at[t_of(dx, dz), 1 - c], s_recv.at[dx, dz])

    def convert(tt, cc):
        rows = pl.ds(pl.multiple_of(cc * 256, 256), 256)
        v = xc[tt, cc, 0]
        hi, lo = split(v)
        xh[tt, rows, :] = hi
        xl[tt, rows, :] = lo
        hi, lo = split(jnp.transpose(v))
        xth[tt, :, rows] = hi
        xtl[tt, :, rows] = lo
        hi, lo = split(xc[tt, cc, 1])
        ch[tt, rows, :] = hi
        cl[tt, rows, :] = lo

    def convert_many(n, where):
        def body(i, carry):
            convert(*where(i))
            return carry

        lax.fori_loop(0, n, body, 0)

    for k in range(3):
        wait(w.at[y, k], w_recv.at[k])
        y_send_step(1, k)
        if k == 0:
            from_right(0)
            from_left(0)
    a_wait(0, 1)
    b = xc.at[t_of(0, 1), c]
    remote(b, b, a_send.at[4], a_recv.at[3, 1], xr)
    remote(b, b, a_send.at[5], a_recv.at[1, 1], xleft)
    to_sibling(0, 1)
    for k in range(3):
        y_wait_step(1, k)
        y_send_step(2, k)
    from_right(1)
    from_left(1)
    a_wait(2, 0)
    to_sibling(2, 0)
    pltpu.make_async_copy(xc.at[own, c], xc.at[own, c], own_sem).wait()
    s_wait(0, 0)
    s_wait(1, 0)
    s_wait(3, 0)
    convert_many(6, lambda i: (lax.rem(x + 3 + i // 2, NX) * NZL + zl, lax.rem(i, 2)))
    for k in range(3):
        y_wait_step(2, k)
        y_send_step(3, k)
    a_wait(2, 1)
    to_sibling(2, 1)
    for dx, dz in ((0, 1), (1, 1), (3, 1), (2, 0)):
        s_wait(dx, dz)
    convert_many(6, lambda i: (lax.rem(x + 3 + i // 2, NX) * NZL + 1 - zl, lax.rem(i, 2)))
    convert_many(2, lambda i: (lax.rem(x + 2, NX) * NZL + zl, i))
    s_wait(2, 1)
    convert_many(2, lambda i: (lax.rem(x + 2, NX) * NZL + 1 - zl, i))

    lhs = ((ch, cl), (xh, xl), (xh, xl))

    def forward(bs, k, first=False):
        n = 128 * len(bs)
        for i, b in enumerate(bs):
            hi, lo = split(w[b, k])
            wh[pl.ds(i * 128, 128), :] = hi
            wl[pl.ds(i * 128, 128), :] = lo
        ah, al = lhs[k]

        def body(r, carry):
            rows = pl.ds(pl.multiple_of(r * 256, 256), 256)
            if len(bs) == 2:
                h = jnp.concatenate([ah[b, rows, :] for b in bs], axis=1)
                l = jnp.concatenate([al[b, rows, :] for b in bs], axis=1)
            else:
                h = ah[bs[0], rows, :]
                l = al[bs[0], rows, :]
            v = dot3(h, l, wh[pl.ds(0, n), :], wl[pl.ds(0, n), :])
            if first:
                acc[k, rows, :] = v
            else:
                acc[k, rows, :] += v
            return carry

        lax.fori_loop(0, 2, body, 0)

    for k in range(3):
        forward((y,), k, True)
    for k in range(3):
        forward((y_of(1), y_of(7)), k)
    for k in range(3):
        y_wait_step(3, k)
        y_send_step(4, k)
    for k in range(3):
        forward((y_of(2), y_of(6)), k)
    for k in range(3):
        forward((y_of(3), y_of(5)), k)
    for k in range(3):
        y_wait_step(4, k)
        forward((y_of(4),), k)

    def rows_body(r, carry):
        rows = pl.ds(pl.multiple_of(r * 64, 64), 64)
        back = acc[0, rows, :]
        gate = acc[1, rows, :]
        lift = acc[2, rows, :]
        s = 1.0 / (1.0 + jnp.exp(-gate))
        bs = back * s
        hi, lo = split(bs * lift * (1.0 + gate * (1.0 - s)))
        rh[rows, 0:256] = hi
        rl[rows, 0:256] = lo
        hi, lo = split(bs * gate)
        rh[rows, 256:512] = hi
        rl[rows, 256:512] = lo
        return carry

    lax.fori_loop(0, 8, rows_body, 0)

    def backward(bs, m):
        if len(bs) == 2:
            h = jnp.concatenate([xth[b] for b in bs], axis=0)
            l = jnp.concatenate([xtl[b] for b in bs], axis=0)
        else:
            h, l = xth[bs[0]], xtl[bs[0]]
        cols = pl.ds(m * 256, 256)
        v = dot3(h, l, rh[:, cols], rl[:, cols])
        for i, b in enumerate(bs):
            gbuf[b, m] = v[i * 128 : (i + 1) * 128]

    def r_step(s, m):
        if s == 1:
            b = y_of(4)
            for d, dev in ((0, yr), (1, yl)):
                half = pl.ds(64 * d, 64)
                remote(
                    gbuf.at[b, m, half, :], rbuf.at[d, 0, m, half, :],
                    r_send.at[d, 0, m], r_recv.at[d, 0, m], dev,
                )
            return
        for d, dev in ((0, yr), (1, yl)):
            b = y_of(5 - s) if d == 0 else y_of(3 + s)
            if s == 2:
                half = pl.ds(64 * d, 64)
                wait(rbuf.at[d, 0, m, half, :], r_recv.at[d, 0, m])
                gbuf[b, m, half, :] += rbuf[d, 0, m, half, :]
            else:
                wait(rbuf.at[d, s - 2, m], r_recv.at[d, s - 2, m])
                gbuf[b, m] += rbuf[d, s - 2, m]
            remote(
                gbuf.at[b, m], rbuf.at[d, s - 1, m],
                r_send.at[d, s - 1, m], r_recv.at[d, s - 1, m], dev,
            )

    for m in range(2):
        backward((y_of(4),), m)
        r_step(1, m)
    for m in range(2):
        backward((y_of(3), y_of(5)), m)
    for m in range(2):
        r_step(2, m)
    for m in range(2):
        backward((y_of(2), y_of(6)), m)
    for m in range(2):
        r_step(3, m)
    for m in range(2):
        backward((y_of(1), y_of(7)), m)
    for m in range(2):
        r_step(4, m)
    for m in range(2):
        backward((y,), m)

    for m in range(2):
        wait(rbuf.at[0, 3, m], r_recv.at[0, 3, m])
        wait(rbuf.at[1, 3, m], r_recv.at[1, 3, m])
        for i in range(8):
            rows = pl.ds(16 * i, 16)
            tbuf[i, m] = gbuf[y, m, rows, :] + rbuf[0, 3, m, rows, :] + rbuf[1, 3, m, rows, :]
    src = zh * 2 + c
    for n, (dz, dc) in enumerate(zpeers):
        zz, cc, dev = zc_of(dz, dc)
        remote(tbuf.at[zz * 2 + cc], zbuf.at[src], z_send.at[n], z_recv, dev)
    zbuf[src] = tbuf[src]
    wait(zbuf.at[pl.ds(0, 7)], z_recv)
    for m in range(2):
        for cc in range(2):
            out_ref[m, :, cc * 256 : cc * 256 + 256] = (
                (zbuf[cc, m] + zbuf[2 + cc, m]) + (zbuf[4 + cc, m] + zbuf[6 + cc, m])
            )

    for k in range(3):
        wait(w.at[0, 0, pl.ds(0, 112), :], w_send.at[k])
    for n in range(6):
        wait(xc.at[0, 0], a_send.at[n])
    for n in range(6, 10):
        wait(xc.at[0, 0, 0], a_send.at[n])
    for dx in range(4):
        for dz in range(2):
            if (dx, dz) != (0, 0):
                wait(xc.at[0, 0], s_send.at[dx, dz])
    for d in range(2):
        for k in range(3):
            for s in range(4):
                n = 64 if s == 3 else 128
                wait(w.at[0, 0, pl.ds(0, n), :], y_send.at[d, s, k])
        for m in range(2):
            for s in range(4):
                n = 64 if s == 0 else 128
                wait(gbuf.at[0, 0, pl.ds(0, n), :], r_send.at[d, s, m])
    for n in range(7):
        wait(tbuf.at[0], z_send.at[n])


def grads(inputs, cotangent, gate_weight, up_weight, down_weight):
    dma = pltpu.SemaphoreType.DMA
    return pl.pallas_call(
        kernel,
        name="grads",
        out_shape=jax.ShapeDtypeStruct((2, 16, 512), F32),
        in_specs=[pl.BlockSpec(memory_space=pl.ANY)] * 5,
        out_specs=pl.BlockSpec(memory_space=pltpu.VMEM),
        scratch_shapes=[
            pltpu.VMEM((8, 2, 2, 256, 128), F32),
            pltpu.VMEM((8, 3, 128, 256), F32),
            pltpu.VMEM((8, 512, 128), BF16),
            pltpu.VMEM((8, 512, 128), BF16),
            pltpu.VMEM((8, 512, 128), BF16),
            pltpu.VMEM((8, 512, 128), BF16),
            pltpu.VMEM((8, 128, 512), BF16),
            pltpu.VMEM((8, 128, 512), BF16),
            pltpu.VMEM((256, 256), BF16),
            pltpu.VMEM((256, 256), BF16),
            pltpu.VMEM((3, 512, 256), F32),
            pltpu.VMEM((512, 512), BF16),
            pltpu.VMEM((512, 512), BF16),
            pltpu.VMEM((8, 2, 128, 256), F32),
            pltpu.VMEM((2, 4, 2, 128, 256), F32),
            pltpu.VMEM((8, 2, 16, 256), F32),
            pltpu.VMEM((8, 2, 16, 256), F32),
            dma,
            dma((4, 2)),
            dma((10,)),
            dma((4, 2)),
            dma((4, 2)),
            dma((3,)),
            dma((3,)),
            dma((2, 4, 3)),
            dma((2, 4, 3)),
            dma((2, 4, 2)),
            dma((2, 4, 2)),
            dma,
            dma((7,)),
        ],
        compiler_params=pltpu.CompilerParams(
            collective_id=0, has_side_effects=True, vmem_limit_bytes=48 * 1024 * 1024
        ),
    )(inputs, cotangent, gate_weight, up_weight, down_weight)


def local(
    inputs,
    cotangent,
    gate_weight,
    up_weight,
    down_weight,
    gate_first,
    gate_second,
    up_first,
    up_second,
):
    g = grads(inputs, cotangent, gate_weight, up_weight, down_weight)
    gate_new, gate_first_new, gate_second_new = adam_update(
        gate_weight, gate_first, gate_second, g[0]
    )
    up_new, up_first_new, up_second_new = adam_update(up_weight, up_first, up_second, g[1])
    return (gate_new, gate_first_new, gate_second_new, up_new, up_first_new, up_second_new)


def solution(mesh):
    spec = P("dp", "tensor")
    return jax.shard_map(
        local, mesh=mesh, in_specs=(spec,) * 9, out_specs=(spec,) * 6, check_vma=False
    )
```

time: 683 us -> 96.2 us (0.14)
  waiting for transfers between devices: 641 us -> 0 us
  Pallas kernels: 0 us -> 90.4 us
  matrix products: 16.1 us -> 0 us
  between operations: 14.2 us -> 0.69 us
    all_gather x5 -> x0, waiting for transfers between devices: 345 us -> none  [the longest x1 94.2 us: local(): lax.all_gather(down_weight, 'dp', axis=0, tiled=True)]
    reduce_scatter x2 -> x0, waiting for transfers between devices: 293 us -> none  [the longest x1 152 us: local(): lax.psum_scatter(make_term(gate_rows), 'dp', scatter_dimension=0, tiled=T...]
    pallas_call x0 -> x1, Pallas kernels: none -> 90.4 us  [grads(): pl.pallas_call(kernel, name='grads', out_shape=jax.ShapeDtypeStruct((2, 1...]
    dot_general x5 -> x0, matrix products: 16.1 us -> none  [the longest x3 12.2 us: contract(): jnp.dot(left, piece, precision=lax.Precision.HIGHEST, preferred_element_t...]
  transfers between devices with their start and end apart: 7 -> 0, of which waited for: 7 -> 0; matrix products, arithmetic and copies ran while one was open for 3% -> 0% of each run, Pallas kernels for 0% -> 0%
where the time goes in v1:
time: 96.2 us; the launch traced here: 95.8 us
  Pallas kernels  90.4 us (94%)
  local copies, waits for them, and re-layouts  4.09 us (4%)
    pallas_call x1, Pallas kernels, grads(): pl.pallas_call(kernel, name='grads', out_shape=jax.ShapeDtypeStruct((2, 1...  90.4 us
    unnamed x18, local copies, waits for them, and re-layouts  4.09 us

profile of v1, /device:TPU:1, one launch (start us, length us, event | category | flops | bytes accessed | tf_op | source)
XLA Modules:
  0.0 95.8 jit_solution(4374124338514790361)
XLA Ops:
  0.6 0.0 copy-start
  0.6 0.7 copy-done
  1.4 0.0 copy-start.1
  1.4 0.8 copy-done.1
  2.2 0.0 copy-start.2
  2.2 0.9 copy-done.2
  3.1 0.0 copy-start.3
  3.1 0.9 copy-done.3
  4.0 0.0 copy-start.4
  4.0 0.8 copy-done.4
  4.7 0.0 copy-start.5
  4.7 0.0 copy-start.6
  4.7 0.0 copy-start.7
  4.7 0.0 copy-start.8
  4.7 90.4 %grads.1 = f32[2,16,512]{2,1,0:T(8,128)S(1)} custom-call(f32[256,128]{1,0:T(8,128)S(1)} %copy-done.2, f32[256,128]{1,0:T(8,128)S(1)} %copy-done.3, f32[16,512]{1,0:T(8,128)S(1)} %copy-done.1, f32[16,512]{1,0:T(8,128)S(1)} %copy-done, f32[16,512]{1,0:T(8,128)S(1)} %copy-done.4), custom_call_target="tpu_custom_call" | custom-call | tf_op jit(solution)/shard_map/grads/pallas_call | solution.py:380
  95.1 0.0 copy-done.5
  95.1 0.0 copy-done.6
  95.1 0.0 copy-done.7
  95.1 0.0 copy-done.8
  95.1 0.7 divide_subtract_fusion
Async XLA Ops:
  0.6 0.8 copy-start
  1.4 0.8 copy-start.1
  2.2 0.9 copy-start.2
  3.1 0.9 copy-start.3
  4.0 0.8 copy-start.4
  4.7 90.4 %copy-start.5 = (f32[16,512]{1,0:T(8,128)S(1)}, f32[16,512]{1,0:T(8,128)}, u32[]{:S(2)}) copy-start(f32[16,512]{1,0:T(8,128)} %param.16) | copy-start | bytes 98308
  4.7 90.4 %copy-start.6 = (f32[16,512]{1,0:T(8,128)S(1)}, f32[16,512]{1,0:T(8,128)}, u32[]{:S(2)}) copy-start(f32[16,512]{1,0:T(8,128)} %param.17) | copy-start | bytes 98308
  4.7 90.4 %copy-start.7 = (f32[16,512]{1,0:T(8,128)S(1)}, f32[16,512]{1,0:T(8,128)}, u32[]{:S(2)}) copy-start(f32[16,512]{1,0:T(8,128)} %param.15) | copy-start | bytes 98308
  4.7 90.4 %copy-start.8 = (f32[16,512]{1,0:T(8,128)S(1)}, f32[16,512]{1,0:T(8,128)}, u32[]{:S(2)}) copy-start(f32[16,512]{1,0:T(8,128)} %param.14) | copy-start | bytes 98308

commit v2 on v1

--- a/solution.py
+++ b/solution.py
@@ -38,7 +38,7 @@
     in_ref, cot_ref, gw_ref, uw_ref, dw_ref, out_ref,
     xc, w, xh, xl, ch, cl, xth, xtl, wh, wl, acc, rh, rl, gbuf, rbuf, tbuf, zbuf,
     own_sem, a_recv, a_send, s_recv, s_send, w_recv, w_send, y_recv, y_send,
-    r_recv, r_send, z_recv, z_send,
+    u_recv, u_send, uy_recv, uy_send, uz_recv, uz_send, r_recv, r_send, z_recv, z_send,
 ):
     dp = lax.axis_index("dp")
     t = lax.axis_index("tensor")
@@ -87,7 +87,7 @@
     def wait(ref, sem):
         pltpu.make_async_copy(ref, ref, sem).wait()
 
-    w_srcs = (dw_ref, gw_ref, uw_ref)
+    w_srcs = (dw_ref, gw_ref)
 
     def w_first(k):
         row = pl.multiple_of(zh * 32 + c * 16, 16)
@@ -112,12 +112,58 @@
         for j, src in enumerate((in_ref, cot_ref)):
             remote(src, xc.at[own, c, j], send.at[n], recv, dev)
 
+    def zrows(zz, first=0, n=32):
+        return pl.ds(pl.multiple_of(zz * 32 + first, 16), n)
+
+    zr, zleft = zc_of(1, 0)[2], zc_of(3, 0)[2]
+    zat = [lax.rem(zh + d, NZH) for d in range(NZH)]
+
+    def u_first():
+        mine = zrows(zh, c * 16, 16)
+        col = pl.multiple_of((1 - c) * 256, 256)
+        remote(uw_ref.at[:, pl.ds(col, 256)], w.at[y, 2, mine, :], u_send, u_recv, sib)
+        col = pl.multiple_of(c * 256, 256)
+        pltpu.make_async_copy(uw_ref.at[:, pl.ds(col, 256)], w.at[y, 2, mine, :], u_recv).start()
+
+    def u_parts(s, back):
+        if s < 4:
+            lo, hi = y_of((9 - s - back) % 8), y_of(s - 1 + back)
+            return (w.at[lo, 2, zrows(zh), :], w.at[hi, 2, zrows(zh), :])
+        lo, hi = y_of(5 - back), y_of(3 + back)
+        return (w.at[lo, 2, zrows(zh, 0, 16), :], w.at[hi, 2, zrows(zh, 16, 16), :])
+
+    def u_y_send(s):
+        for d, r in enumerate(u_parts(s, 0)):
+            remote(r, r, uy_send.at[d, s - 1], uy_recv.at[d, s - 1], (yr, yl)[d])
+
+    def u_y_wait(s):
+        for d, r in enumerate(u_parts(s, 1)):
+            wait(r, uy_recv.at[d, s - 1])
+
+    def u_group(g, zz, first=0, n=32):
+        return w.at[pl.ds(2 * g, 2), 2, zrows(zz, first, n), :]
+
+    def u_z_send(g):
+        r = u_group(g, zh)
+        for d in range(2):
+            remote(r, r, uz_send.at[0, d, g], uz_recv.at[0, d, g], (zr, zleft)[d])
+
+    def u_z_relay(g):
+        for d, zz in enumerate((zat[3], zat[1])):
+            wait(u_group(g, zz), uz_recv.at[0, d, g])
+            r = u_group(g, zz, 16 * d, 16)
+            remote(r, r, uz_send.at[1, d, g], uz_recv.at[1, d, g], (zr, zleft)[d])
+
+    def u_z_end(g):
+        for d in range(2):
+            wait(u_group(g, zat[2], 16 * d, 16), uz_recv.at[1, d, g])
+
     w_first(0)
     own_rows(0, xr, a_send, a_recv.at[3, 0])
     own_rows(1, xleft, a_send, a_recv.at[1, 0])
+    u_first()
+    w_first(1)
     own_rows(2, zpart, a_send, a_recv.at[0, 1])
-    w_first(1)
-    w_first(2)
     own_rows(3, sib, a_send, s_recv.at[0, 0])
     for j, src in enumerate((in_ref, cot_ref)):
         pltpu.make_async_copy(src, xc.at[own, c, j], own_sem).start()
@@ -187,38 +233,58 @@
 
         lax.fori_loop(0, n, body, 0)
 
-    for k in range(3):
-        wait(w.at[y, k], w_recv.at[k])
-        y_send_step(1, k)
-        if k == 0:
-            from_right(0)
-            from_left(0)
+    def y_next(s, k):
+        y_wait_step(s, k)
+        y_send_step(s + 1, k)
+
+    wait(w.at[y, 2, zrows(zh), :], u_recv)
+    u_y_send(1)
+    for s in range(1, 3):
+        u_y_wait(s)
+        u_y_send(s + 1)
+    wait(w.at[y, 0], w_recv.at[0])
+    y_send_step(1, 0)
+    from_right(0)
+    from_left(0)
+    u_y_wait(3)
+    u_y_send(4)
+    wait(w.at[y, 1], w_recv.at[1])
+    y_send_step(1, 1)
+    u_y_wait(4)
+    for g in range(4):
+        u_z_send(g)
+    y_next(1, 0)
     a_wait(0, 1)
     b = xc.at[t_of(0, 1), c]
     remote(b, b, a_send.at[4], a_recv.at[3, 1], xr)
     remote(b, b, a_send.at[5], a_recv.at[1, 1], xleft)
     to_sibling(0, 1)
-    for k in range(3):
-        y_wait_step(1, k)
-        y_send_step(2, k)
-    from_right(1)
-    from_left(1)
     a_wait(2, 0)
     to_sibling(2, 0)
+    y_next(1, 1)
     pltpu.make_async_copy(xc.at[own, c], xc.at[own, c], own_sem).wait()
     s_wait(0, 0)
     s_wait(1, 0)
     s_wait(3, 0)
     convert_many(6, lambda i: (lax.rem(x + 3 + i // 2, NX) * NZL + zl, lax.rem(i, 2)))
-    for k in range(3):
-        y_wait_step(2, k)
-        y_send_step(3, k)
+    u_z_relay(0)
+    y_next(2, 0)
+    s_wait(0, 1)
+    s_wait(2, 0)
+    convert_many(2, lambda i: (x * NZL + 1 - zl, i))
+    convert_many(2, lambda i: (lax.rem(x + 2, NX) * NZL + zl, i))
+    y_next(2, 1)
+    from_right(1)
+    from_left(1)
+    u_z_relay(1)
+    y_next(3, 0)
+    s_wait(1, 1)
+    s_wait(3, 1)
+    convert_many(4, lambda i: (lax.rem(x + 3 + 2 * (i // 2), NX) * NZL + 1 - zl, lax.rem(i, 2)))
+    u_z_relay(2)
     a_wait(2, 1)
     to_sibling(2, 1)
-    for dx, dz in ((0, 1), (1, 1), (3, 1), (2, 0)):
-        s_wait(dx, dz)
-    convert_many(6, lambda i: (lax.rem(x + 3 + i // 2, NX) * NZL + 1 - zl, lax.rem(i, 2)))
-    convert_many(2, lambda i: (lax.rem(x + 2, NX) * NZL + zl, i))
+    y_next(3, 1)
     s_wait(2, 1)
     convert_many(2, lambda i: (lax.rem(x + 2, NX) * NZL + 1 - zl, i))
 
@@ -249,20 +315,18 @@
 
         lax.fori_loop(0, 2, body, 0)
 
-    for k in range(3):
+    for k in range(2):
         forward((y,), k, True)
-    for k in range(3):
-        forward((y_of(1), y_of(7)), k)
-    for k in range(3):
-        y_wait_step(3, k)
-        y_send_step(4, k)
-    for k in range(3):
-        forward((y_of(2), y_of(6)), k)
-    for k in range(3):
-        forward((y_of(3), y_of(5)), k)
-    for k in range(3):
+    u_z_relay(3)
+    for d in range(1, 4):
+        for k in range(2):
+            forward((y_of(d), y_of(8 - d)), k)
+    for k in range(2):
         y_wait_step(4, k)
         forward((y_of(4),), k)
+    for g in range(4):
+        u_z_end(g)
+        forward((2 * g, 2 * g + 1), 2, g == 0)
 
     def rows_body(r, carry):
         rows = pl.ds(pl.multiple_of(r * 64, 64), 64)
@@ -334,26 +398,27 @@
     for m in range(2):
         backward((y,), m)
 
+    src = zh * 2 + c
     for m in range(2):
         wait(rbuf.at[0, 3, m], r_recv.at[0, 3, m])
         wait(rbuf.at[1, 3, m], r_recv.at[1, 3, m])
         for i in range(8):
             rows = pl.ds(16 * i, 16)
-            tbuf[i, m] = gbuf[y, m, rows, :] + rbuf[0, 3, m, rows, :] + rbuf[1, 3, m, rows, :]
-    src = zh * 2 + c
-    for n, (dz, dc) in enumerate(zpeers):
-        zz, cc, dev = zc_of(dz, dc)
-        remote(tbuf.at[zz * 2 + cc], zbuf.at[src], z_send.at[n], z_recv, dev)
-    zbuf[src] = tbuf[src]
-    wait(zbuf.at[pl.ds(0, 7)], z_recv)
-    for m in range(2):
+            tbuf[m, i] = gbuf[y, m, rows, :] + rbuf[0, 3, m, rows, :] + rbuf[1, 3, m, rows, :]
+        for n, (dz, dc) in enumerate(zpeers):
+            zz, cc, dev = zc_of(dz, dc)
+            remote(tbuf.at[m, zz * 2 + cc], zbuf.at[m, src], z_send.at[m, n], z_recv.at[m], dev)
+        zbuf[m, src] = tbuf[m, src]
+    for m in range(2):
+        wait(zbuf.at[m, pl.ds(0, 7)], z_recv.at[m])
         for cc in range(2):
             out_ref[m, :, cc * 256 : cc * 256 + 256] = (
-                (zbuf[cc, m] + zbuf[2 + cc, m]) + (zbuf[4 + cc, m] + zbuf[6 + cc, m])
+                (zbuf[m, cc] + zbuf[m, 2 + cc]) + (zbuf[m, 4 + cc] + zbuf[m, 6 + cc])
             )
 
-    for k in range(3):
+    for k in range(2):
         wait(w.at[0, 0, pl.ds(0, 112), :], w_send.at[k])
+    wait(w.at[0, 0, pl.ds(0, 16), :], u_send)
     for n in range(6):
         wait(xc.at[0, 0], a_send.at[n])
     for n in range(6, 10):
@@ -363,16 +428,23 @@
             if (dx, dz) != (0, 0):
                 wait(xc.at[0, 0], s_send.at[dx, dz])
     for d in range(2):
-        for k in range(3):
+        for k in range(2):
             for s in range(4):
                 n = 64 if s == 3 else 128
                 wait(w.at[0, 0, pl.ds(0, n), :], y_send.at[d, s, k])
+        for s in range(4):
+            n = 16 if s == 3 else 32
+            wait(w.at[0, 0, pl.ds(0, n), :], uy_send.at[d, s])
+        for g in range(4):
+            wait(w.at[0, 0, pl.ds(0, 64), :], uz_send.at[0, d, g])
+            wait(w.at[0, 0, pl.ds(0, 32), :], uz_send.at[1, d, g])
         for m in range(2):
             for s in range(4):
                 n = 64 if s == 0 else 128
                 wait(gbuf.at[0, 0, pl.ds(0, n), :], r_send.at[d, s, m])
-    for n in range(7):
-        wait(tbuf.at[0], z_send.at[n])
+    for m in range(2):
+        for n in range(7):
+            wait(tbuf.at[0, 0], z_send.at[m, n])
 
 
 def grads(inputs, cotangent, gate_weight, up_weight, down_weight):
@@ -399,24 +471,30 @@
             pltpu.VMEM((512, 512), BF16),
             pltpu.VMEM((8, 2, 128, 256), F32),
             pltpu.VMEM((2, 4, 2, 128, 256), F32),
-            pltpu.VMEM((8, 2, 16, 256), F32),
-            pltpu.VMEM((8, 2, 16, 256), F32),
+            pltpu.VMEM((2, 8, 16, 256), F32),
+            pltpu.VMEM((2, 8, 16, 256), F32),
             dma,
             dma((4, 2)),
             dma((10,)),
             dma((4, 2)),
             dma((4, 2)),
-            dma((3,)),
-            dma((3,)),
-            dma((2, 4, 3)),
-            dma((2, 4, 3)),
+            dma((2,)),
+            dma((2,)),
             dma((2, 4, 2)),
             dma((2, 4, 2)),
             dma,
-            dma((7,)),
+            dma,
+            dma((2, 4)),
+            dma((2, 4)),
+            dma((2, 2, 4)),
+            dma((2, 2, 4)),
+            dma((2, 4, 2)),
+            dma((2, 4, 2)),
+            dma((2,)),
+            dma((2, 7)),
         ],
         compiler_params=pltpu.CompilerParams(
-            collective_id=0, has_side_effects=True, vmem_limit_bytes=48 * 1024 * 1024
+            collective_id=0, has_side_effects=True, vmem_limit_bytes=67043328
         ),
     )(inputs, cotangent, gate_weight, up_weight, down_weight)
 

time: 96.2 us -> 85.9 us (0.89)
  Pallas kernels: 90.4 us -> 83.4 us
  local copies, waits for them, and re-layouts: 4.09 us -> 0 us
    pallas_call x1, Pallas kernels: 90.4 us -> 83.4 us  [grads(): pl.pallas_call(kernel, name='grads', out_shape=jax.ShapeDtypeStruct((2, 1...]
    unnamed x18 -> x0, local copies, waits for them, and re-layouts: 4.09 us -> none
where the time goes in v2:
time: 85.9 us; the launch traced here: 85.7 us
  Pallas kernels  83.4 us (97%)
  other arithmetic  1.57 us (2%)
    pallas_call x1, Pallas kernels, grads(): pl.pallas_call(kernel, name='grads', out_shape=jax.ShapeDtypeStruct((2, 1...  83.4 us

profile of v2, /device:TPU:1, one launch (start us, length us, event | category | flops | bytes accessed | tf_op | source)
XLA Modules:
  0.0 85.7 jit_solution(9318485435727810179)
XLA Ops:
  0.6 83.4 %grads.1 = f32[2,16,512]{2,1,0:T(8,128)} custom-call(f32[256,128]{1,0:T(8,128)} %in_ref.1, f32[256,128]{1,0:T(8,128)} %cot_ref.1, f32[16,512]{1,0:T(8,128)} %gw_ref.1, f32[16,512]{1,0:T(8,128)} %uw_ref.1, f32[16,512]{1,0:T(8,128)} %dw_ref.1), custom_call_target="tpu_custom_call" | custom-call | tf_op jit(solution)/shard_map/grads/pallas_call | solution.py:452
  84.1 1.6 %divide_subtract_fusion = (f32[16,512]{1,0:T(8,128)}, f32[16,512]{1,0:T(8,128)}, f32[16,512]{1,0:T(8,128)}, f32[16,512]{1,0:T(8,128)}, f32[16,512]{1,0:T(8,128)}, /*index=5*/f32[16,512]{1,0:T(8,128)}) fusion(f32[16,512]{1,0:T(8,128)} %uw_ref.1, f32[2,16,512]{2,1,0:T(8,128)} %grads.1, f32[16,512]{1,0:T(8,128)} %param.16, f32[16,512]{1,0:T(8,128)} %param.17, ...), kind=kLoop, calls=%fused_computation.8 | loop fusion | flops 196608 | bytes 458752 | tf_op jit(solution)/shard_map/sub | solution.py:20

commit v3 on v0

v3 whole, which is shorter than its diff:
```python
import jax
import jax.numpy as jnp
from jax import lax
from jax.experimental import pallas as pl
from jax.experimental.pallas import tpu as pltpu
from jax.sharding import PartitionSpec as P

STEP = 100
MESH = pl.DeviceIdType.MESH
F32 = jnp.float32
BF16 = jnp.bfloat16
NX, NZL, NY, NZH = 4, 2, 8, 4


def adam_update(weight, first, second, grad):
    first_new = 0.9 * first + 0.1 * grad
    second_new = 0.95 * second + 0.05 * grad * grad
    first_hat = first_new / (1.0 - 0.9**STEP)
    second_hat = second_new / (1.0 - 0.95**STEP)
    weight_new = weight - 0.003 * first_hat / (jnp.sqrt(second_hat) + 1e-08)
    return (weight_new, first_new, second_new)


def split(v):
    hi = v.astype(BF16)
    return hi, (v - hi.astype(F32)).astype(BF16)


def dot(a, b):
    return jnp.dot(a, b, preferred_element_type=F32)


def dot3(ah, al, bh, bl):
    return dot(ah, bh) + dot(ah, bl) + dot(al, bh)


def kernel(
    in_ref, cot_ref, gw_ref, uw_ref, dw_ref, out_ref,
    xc, w, xh, xl, ch, cl, xth, xtl, acc, rh, rl,
    gbuf, rbuf, tbuf, zbuf, gz, rz1, rz2, yz,
    own_sem, a_recv, a_send, s_recv, s_send, o_recv, o_send, w_recv, w_send, y_recv, y_send,
    u_recv, u_send, r_recv, r_send, z_recv, z_send, f_recv, f_send, g_recv, g_send,
):
    dp = lax.axis_index("dp")
    t = lax.axis_index("tensor")
    c = lax.rem(dp, 2)
    zh = lax.rem(dp // 2, NZH)
    y = dp // (2 * NZH)
    x = t // NZL
    zl = lax.rem(t, NZL)

    def t_of(dx, dz):
        zz = zl if dz == 0 else 1 - zl
        return lax.rem(x + dx, NX) * NZL + zz

    def y_of(d):
        return lax.rem(y + d, NY)

    def core_of(dc):
        return c if dc == 0 else 1 - c

    def dev_of(dy, dz, dc):
        return ((y_of(dy) * NZH + zat[dz]) * 2 + core_of(dc), t)

    zat = [lax.rem(zh + d, NZH) for d in range(NZH)]
    sib = dev_of(0, 0, 1)
    zpart = (dp, t_of(0, 1))
    xs = ((dp, t_of(1, 0)), (dp, t_of(3, 0)))
    ys = (dev_of(1, 0, 0), dev_of(7, 0, 0))
    zs = (dev_of(0, 1, 0), dev_of(0, 3, 0))
    zpeers = [(2, 0), (2, 1), (1, 0), (3, 0), (1, 1), (3, 1)]
    ypeers = [(dy, dc) for dy in (4, 3, 5, 2, 6, 1, 7) for dc in range(2)]

    barrier = pltpu.get_barrier_semaphore()
    peers = [dev_of(0, dz, dc) for dz, dc in zpeers] + [sib, zpart, xs[0], xs[1]]
    peers = peers + [dev_of(dy, 0, dc) for dy, dc in ypeers]
    for peer in peers:
        pl.semaphore_signal(barrier, inc=1, device_id=peer, device_id_type=MESH)
    pl.semaphore_wait(barrier, len(peers))

    def remote(src, dst, send, recv, dev):
        pltpu.make_async_remote_copy(
            src_ref=src, dst_ref=dst, send_sem=send, recv_sem=recv,
            device_id=dev, device_id_type=MESH,
        ).start()

    def local_copy(src, dst, sem):
        pltpu.make_async_copy(src, dst, sem).start()

    def wait(ref, sem):
        pltpu.make_async_copy(ref, ref, sem).wait()

    w_srcs = (dw_ref, gw_ref, uw_ref)

    def w_own(k):
        mine = pl.ds(pl.multiple_of(c * 16, 16), 16)
        n = k // 2
        there = pl.ds(pl.multiple_of((1 - c) * 256, 256), 256)
        remote(w_srcs[k].at[:, there], w.at[y, k, mine, :], o_send.at[n], o_recv.at[n], sib)
        here = pl.ds(pl.multiple_of(c * 256, 256), 256)
        local_copy(w_srcs[k].at[:, here], w.at[y, k, mine, :], o_recv.at[n])

    def w_first(k):
        for dz, dc in zpeers:
            src = w_srcs[k].at[:, pl.ds(pl.multiple_of(core_of(dc) * 256, 256), 256)]
            rows = pl.ds(pl.multiple_of((4 - dz) * 32 + c * 16, 16), 16)
            remote(src, w.at[y, k, rows, :], w_send.at[k], w_recv.at[k], dev_of(0, dz, dc))

    U, A, B0, B1 = range(4)

    def part(ring, b, half):
        if ring == A:
            return w.at[b, pl.ds(0, 2), pl.ds(0, 32), :] if half is None else w.at[b, half, pl.ds(0, 32), :]
        k = (2, 0, 0, 1)[ring]
        first, n = (0, 32) if ring == U else (32, 96)
        if half is not None:
            n = n // 2
            first = first + half * n
        return w.at[b, k, pl.ds(first, n), :]

    def step_parts(ring, s, back):
        if s < 4:
            return part(ring, y_of((9 - s - back) % 8), None), part(ring, y_of(s - 1 + back), None)
        return part(ring, y_of(5 - back), 0), part(ring, y_of(3 + back), 1)

    def y_start(ring, s):
        for d, r in enumerate(step_parts(ring, s, 0)):
            remote(r, r, y_send.at[d, s - 1, ring], y_recv.at[d, s - 1, ring], ys[d])

    def y_end(ring, s):
        for d, r in enumerate(step_parts(ring, s, 1)):
            wait(r, y_recv.at[d, s - 1, ring])

    def y_next(ring, s):
        y_end(ring, s)
        y_start(ring, s + 1)

    def u_start(i):
        b = y_of(i)
        for d, first in enumerate((96, 32)):
            remote(
                w.at[b, 2, pl.ds(0, 32), :], w.at[b, 2, pl.ds(first, 32), :],
                u_send.at[0, d, i], u_recv.at[0, d, i], zs[d],
            )

    def u_relay(i):
        b = y_of(i)
        for d, (first, src, dst) in enumerate(((96, 96, 64), (32, 48, 80))):
            wait(w.at[b, 2, pl.ds(first, 32), :], u_recv.at[0, d, i])
            remote(
                w.at[b, 2, pl.ds(src, 16), :], w.at[b, 2, pl.ds(dst, 16), :],
                u_send.at[1, d, i], u_recv.at[1, d, i], zs[d],
            )

    def u_end(i):
        for d in range(2):
            wait(w.at[y_of(i), 2, pl.ds(64 + 16 * d, 16), :], u_recv.at[1, d, i])

    own = t_of(0, 0)
    rows_src = (in_ref, cot_ref)

    def own_to(n, j, dev, recv):
        remote(rows_src[j], xc.at[own, c, j], a_send.at[n + j], recv, dev)

    def pass_on(n, dx, dz, j, d, to_dx):
        b = xc.at[t_of(dx, dz), c, j]
        remote(b, b, a_send.at[n], a_recv.at[to_dx, dz, j], xs[d])

    def a_end(dx, dz, j):
        wait(xc.at[t_of(dx, dz), c, j], a_recv.at[dx, dz, j])

    def from_right(dz):
        a_end(1, dz, 1)
        pass_on(10 + dz, 1, dz, 1, 1, 2)

    def from_left(dz):
        a_end(3, dz, 0)
        pass_on(12 + dz, 3, dz, 0, 0, 2)

    def to_sibling(dx, dz):
        b = xc.at[t_of(dx, dz), c]
        remote(b, b, s_send.at[dx, dz], s_recv.at[dx, dz], sib)

    def s_end(dx, dz):
        wait(xc.at[t_of(dx, dz), 1 - c], s_recv.at[dx, dz])

    def convert(tt, cc):
        rows = pl.ds(pl.multiple_of(cc * 256, 256), 256)
        v = xc[tt, cc, 0]
        hi, lo = split(v)
        xh[tt, rows, :] = hi
        xl[tt, rows, :] = lo
        hi, lo = split(jnp.transpose(v))
        xth[tt, :, rows] = hi
        xtl[tt, :, rows] = lo
        hi, lo = split(xc[tt, cc, 1])
        ch[tt, rows, :] = hi
        cl[tt, rows, :] = lo

    def convert_many(n, where):
        def body(i, carry):
            convert(*where(i))
            return carry

        lax.fori_loop(0, n, body, 0)

    lhs = ((ch, cl), (xh, xl), (xh, xl))
    w_rows = [pl.ds(pl.multiple_of(lax.rem(j + NZH - zh, NZH) * 32, 32), 32) for j in range(NZH)]

    def forward(bs, k, first=False):
        wh, wl = split(jnp.concatenate([w[b, k, r, :] for b in bs for r in w_rows], axis=0))
        ah, al = lhs[k]
        if len(bs) == 2:
            h = jnp.concatenate([ah[b] for b in bs], axis=1)
            l = jnp.concatenate([al[b] for b in bs], axis=1)
        else:
            h, l = ah[bs[0]], al[bs[0]]
        v = dot3(h, l, wh, wl)
        if first:
            acc[k] = v
        else:
            acc[k] += v

    w_own(2)
    w_own(0)
    w_own(1)
    for j in range(2):
        own_to(0, j, xs[0], a_recv.at[3, 0, j])
        own_to(2, j, xs[1], a_recv.at[1, 0, j])
    w_first(0)
    w_first(1)
    for j in range(2):
        own_to(4, j, zpart, a_recv.at[0, 1, j])
    for j in range(2):
        remote(rows_src[j], xc.at[own, c, j], s_send.at[0, 0], s_recv.at[0, 0], sib)
        local_copy(rows_src[j], xc.at[own, c, j], own_sem)

    wait(part(U, y, None), o_recv.at[1])
    y_start(U, 1)
    u_start(0)
    wait(part(A, y, None), o_recv.at[0])
    y_start(A, 1)
    y_next(U, 1)
    u_start(1)
    u_start(7)
    y_next(A, 1)
    y_next(U, 2)
    u_start(2)
    u_start(6)
    from_left(0)
    wait(part(B0, y, None), w_recv.at[0])
    y_start(B0, 1)
    from_right(0)
    a_end(1, 0, 0)
    to_sibling(1, 0)
    a_end(3, 0, 1)
    to_sibling(3, 0)
    y_next(A, 2)
    y_next(U, 3)
    u_start(3)
    u_start(5)
    wait(part(B1, y, None), w_recv.at[1])
    y_start(B1, 1)
    a_end(0, 1, 0)
    pass_on(6, 0, 1, 0, 0, 3)
    pass_on(8, 0, 1, 0, 1, 1)
    y_next(B0, 1)
    for j in range(2):
        a_end(2, 0, j)
    to_sibling(2, 0)
    y_next(A, 3)
    y_end(U, 4)
    u_start(4)
    a_end(0, 1, 1)
    pass_on(9, 0, 1, 1, 1, 1)
    pass_on(7, 0, 1, 1, 0, 3)
    to_sibling(0, 1)
    wait(xc.at[own, c], own_sem)
    s_end(0, 0)
    s_end(1, 0)
    s_end(3, 0)
    convert_many(6, lambda i: (lax.rem(x + 3 + i // 2, NX) * NZL + zl, lax.rem(i, 2)))
    from_left(1)
    y_next(B1, 1)
    u_relay(0)
    y_next(B0, 2)
    s_end(2, 0)
    convert_many(2, lambda i: (lax.rem(x + 2, NX) * NZL + zl, i))
    s_end(0, 1)
    convert_many(2, lambda i: (x * NZL + 1 - zl, i))
    from_right(1)
    a_end(1, 1, 0)
    to_sibling(1, 1)
    a_end(3, 1, 1)
    to_sibling(3, 1)
    u_relay(1)
    u_relay(7)
    y_next(B1, 2)
    u_relay(2)
    u_relay(6)
    y_next(B0, 3)
    s_end(1, 1)
    s_end(3, 1)
    convert_many(4, lambda i: (lax.rem(x + 3 + 2 * (i // 2), NX) * NZL + 1 - zl, lax.rem(i, 2)))
    for j in range(2):
        a_end(2, 1, j)
    to_sibling(2, 1)
    u_relay(3)
    u_relay(5)
    y_next(B1, 3)
    u_relay(4)
    s_end(2, 1)
    convert_many(2, lambda i: (lax.rem(x + 2, NX) * NZL + 1 - zl, i))
    pairs = [(y_of(d), y_of(8 - d)) for d in range(1, 4)] + [(y, y_of(4))]
    for k in range(2):
        for i in range(3):
            forward(pairs[i], k, i == 0)
    for i in range(3):
        u_end(i + 1)
        u_end(7 - i)
        forward(pairs[i], 2, i == 0)
    y_end(A, 4)
    y_end(B0, 4)
    forward(pairs[3], 0)
    y_end(B1, 4)
    forward(pairs[3], 1)
    u_end(0)
    u_end(4)
    forward(pairs[3], 2)

    def rows_body(r, carry):
        rows = pl.ds(pl.multiple_of(r * 64, 64), 64)
        back = acc[0, rows, :]
        gate = acc[1, rows, :]
        lift = acc[2, rows, :]
        s = 1.0 / (1.0 + jnp.exp(-gate))
        bs = back * s
        hi, lo = split(bs * lift * (1.0 + gate * (1.0 - s)))
        rh[rows, 0:256] = hi
        rl[rows, 0:256] = lo
        hi, lo = split(bs * gate)
        rh[rows, 256:512] = hi
        rl[rows, 256:512] = lo
        return carry

    lax.fori_loop(0, 8, rows_body, 0)

    def backward(bs):
        h = jnp.concatenate([xth[b] for b in bs], axis=0) if len(bs) == 2 else xth[bs[0]]
        l = jnp.concatenate([xtl[b] for b in bs], axis=0) if len(bs) == 2 else xtl[bs[0]]
        v = dot3(h, l, rh[:, 0:384], rl[:, 0:384])
        for i, b in enumerate(bs):
            for q in range(3):
                gbuf[b, q] = v[i * 128 : (i + 1) * 128, q * 128 : (q + 1) * 128]

    def backward_last(i, carry):
        h = jnp.concatenate([xth[2 * i], xth[2 * i + 1]], axis=0)
        l = jnp.concatenate([xtl[2 * i], xtl[2 * i + 1]], axis=0)
        v = dot3(h, l, rh[:, 384:512], rl[:, 384:512])
        gz[2 * i] = v[0:128]
        gz[2 * i + 1] = v[128:256]
        return carry

    def r_start(s, q, d):
        b = y_of(5 - s) if d == 0 else y_of(3 + s)
        rows = pl.ds(64 * d, 64) if s == 1 else pl.ds(0, 128)
        remote(
            gbuf.at[b, q, rows, :], rbuf.at[d, s - 1, q, rows, :],
            r_send.at[d, s - 1, q], r_recv.at[d, s - 1, q], ys[d],
        )

    def r_step(s):
        for q in range(3):
            for d in range(2):
                b = y_of(5 - s) if d == 0 else y_of(3 + s)
                rows = pl.ds(64 * d, 64) if s == 2 else pl.ds(0, 128)
                wait(rbuf.at[d, s - 2, q, rows, :], r_recv.at[d, s - 2, q])
                gbuf[b, q, rows, :] += rbuf[d, s - 2, q, rows, :]
                r_start(s, q, d)

    def z_rows(d, first, n):
        return pl.ds(pl.multiple_of(zat[d] * 32 + first, 16), n)

    backward((y_of(4),))
    for q in range(3):
        for d in range(2):
            r_start(1, q, d)
    lax.fori_loop(0, 4, backward_last, 0)
    for d in range(2):
        remote(gz.at[:, z_rows(2, 16 * d, 16), :], rz1.at[d], f_send.at[0, d], f_recv.at[0, d], zs[d])
    backward((y_of(3), y_of(5)))
    r_step(2)
    backward((y_of(2), y_of(6)))
    for d, dz in ((0, 1), (1, 3)):
        wait(rz1.at[d], f_recv.at[0, d])
        rows = z_rows(dz, 16 * d, 16)
        gz[:, rows, :] = gz[:, rows, :] + rz1[d]
        remote(gz.at[:, z_rows(dz, 0, 32), :], rz2.at[d], f_send.at[1, d], f_recv.at[1, d], zs[d])
    r_step(3)
    backward((y_of(1), y_of(7)))
    r_step(4)
    backward((y,))
    for d in range(2):
        wait(rz2.at[d], f_recv.at[1, d])
    rows = z_rows(0, 0, 32)
    gz[:, rows, :] = gz[:, rows, :] + rz2[0] + rz2[1]
    for dy, dc in ypeers + [(0, 1)]:
        rows = pl.ds(pl.multiple_of(zh * 32 + core_of(dc) * 16, 16), 16)
        remote(gz.at[y_of(dy), rows, :], yz.at[y * 2 + c], g_send, g_recv, dev_of(dy, 0, dc))
    yz[y * 2 + c] = gz[y, pl.ds(pl.multiple_of(zh * 32 + c * 16, 16), 16), :]

    src = zh * 2 + c
    for q in range(3):
        for d in range(2):
            wait(rbuf.at[d, 3, q], r_recv.at[d, 3, q])
        for i in range(8):
            rows = pl.ds(16 * i, 16)
            tbuf[q, i] = gbuf[y, q, rows, :] + rbuf[0, 3, q, rows, :] + rbuf[1, 3, q, rows, :]
        for dz, dc in zpeers + [(0, 1)]:
            remote(
                tbuf.at[q, zat[dz] * 2 + core_of(dc)], zbuf.at[q, src],
                z_send.at[q], z_recv.at[q], dev_of(0, dz, dc),
            )
        zbuf[q, src] = tbuf[q, src]
    wait(yz.at[pl.ds(0, 15)], g_recv)
    for cc in range(2):
        v = yz[cc]
        for i in range(1, NY):
            v = v + yz[2 * i + cc]
        out_ref[1, :, cc * 256 + 128 : cc * 256 + 256] = v
    for q in range(3):
        wait(zbuf.at[q, pl.ds(0, 7)], z_recv.at[q])
        for cc in range(2):
            col = cc * 256 + (q % 2) * 128
            out_ref[q // 2, :, col : col + 128] = (
                (zbuf[q, cc] + zbuf[q, 2 + cc]) + (zbuf[q, 4 + cc] + zbuf[q, 6 + cc])
            )

    def sent(rows, sem):
        wait(w.at[0, 0, pl.ds(0, rows), :], sem)

    sent(32, o_send.at[0])
    sent(16, o_send.at[1])
    sent(96, w_send.at[0])
    sent(96, w_send.at[1])
    for n in range(14):
        sent(128, a_send.at[n])
    for dx in range(4):
        for dz in range(2):
            wait(xc.at[0, 0], s_send.at[dx, dz])
    for d in range(2):
        for s in range(4):
            for ring, rows in ((U, 32), (A, 64), (B0, 96), (B1, 96)):
                sent(rows // 2 if s == 3 else rows, y_send.at[d, s, ring])
            for q in range(3):
                sent(32 if s == 0 else 64, r_send.at[d, s, q])
        for i in range(NY):
            sent(32, u_send.at[0, d, i])
            sent(16, u_send.at[1, d, i])
        sent(64, f_send.at[0, d])
        sent(128, f_send.at[1, d])
    for q in range(3):
        sent(56, z_send.at[q])
    sent(120, g_send)


def grads(inputs, cotangent, gate_weight, up_weight, down_weight):
    dma = pltpu.SemaphoreType.DMA
    return pl.pallas_call(
        kernel,
        name="grads",
        out_shape=jax.ShapeDtypeStruct((2, 16, 512), F32),
        in_specs=[pl.BlockSpec(memory_space=pl.ANY)] * 5,
        out_specs=pl.BlockSpec(memory_space=pltpu.VMEM),
        scratch_shapes=[
            pltpu.VMEM((8, 2, 2, 256, 128), F32),
            pltpu.VMEM((8, 3, 128, 256), F32),
            pltpu.VMEM((8, 512, 128), BF16),
            pltpu.VMEM((8, 512, 128), BF16),
            pltpu.VMEM((8, 512, 128), BF16),
            pltpu.VMEM((8, 512, 128), BF16),
            pltpu.VMEM((8, 128, 512), BF16),
            pltpu.VMEM((8, 128, 512), BF16),
            pltpu.VMEM((3, 512, 256), F32),
            pltpu.VMEM((512, 512), BF16),
            pltpu.VMEM((512, 512), BF16),
            pltpu.VMEM((8, 3, 128, 128), F32),
            pltpu.VMEM((2, 4, 3, 128, 128), F32),
            pltpu.VMEM((3, 8, 16, 128), F32),
            pltpu.VMEM((3, 8, 16, 128), F32),
            pltpu.VMEM((8, 128, 128), F32),
            pltpu.VMEM((2, 8, 16, 128), F32),
            pltpu.VMEM((2, 8, 32, 128), F32),
            pltpu.VMEM((16, 16, 128), F32),
            dma,
            dma((4, 2, 2)),
            dma((14,)),
            dma((4, 2)),
            dma((4, 2)),
            dma((2,)),
            dma((2,)),
            dma((2,)),
            dma((2,)),
            dma((2, 4, 4)),
            dma((2, 4, 4)),
            dma((2, 2, 8)),
            dma((2, 2, 8)),
            dma((2, 4, 3)),
            dma((2, 4, 3)),
            dma((3,)),
            dma((3,)),
            dma((2, 2)),
            dma((2, 2)),
            dma,
            dma,
        ],
        compiler_params=pltpu.CompilerParams(
            collective_id=0, has_side_effects=True, vmem_limit_bytes=66400000
        ),
    )(inputs, cotangent, gate_weight, up_weight, down_weight)


def local(
    inputs,
    cotangent,
    gate_weight,
    up_weight,
    down_weight,
    gate_first,
    gate_second,
    up_first,
    up_second,
):
    g = grads(inputs, cotangent, gate_weight, up_weight, down_weight)
    gate_new, gate_first_new, gate_second_new = adam_update(
        gate_weight, gate_first, gate_second, g[0]
    )
    up_new, up_first_new, up_second_new = adam_update(up_weight, up_first, up_second, g[1])
    return (gate_new, gate_first_new, gate_second_new, up_new, up_first_new, up_second_new)


def solution(mesh):
    spec = P("dp", "tensor")
    return jax.shard_map(
        local, mesh=mesh, in_specs=(spec,) * 9, out_specs=(spec,) * 6, check_vma=False
    )
```

time: 683 us -> 80.2 us (0.12)
  waiting for transfers between devices: 641 us -> 0 us
  Pallas kernels: 0 us -> 77.8 us
  matrix products: 16.1 us -> 0 us
  between operations: 14.2 us -> 0.74 us
    all_gather x5 -> x0, waiting for transfers between devices: 345 us -> none  [the longest x1 94.2 us: local(): lax.all_gather(down_weight, 'dp', axis=0, tiled=True)]
    reduce_scatter x2 -> x0, waiting for transfers between devices: 293 us -> none  [the longest x1 152 us: local(): lax.psum_scatter(make_term(gate_rows), 'dp', scatter_dimension=0, tiled=T...]
    pallas_call x0 -> x1, Pallas kernels: none -> 77.8 us  [grads(): pl.pallas_call(kernel, name='grads', out_shape=jax.ShapeDtypeStruct((2, 1...]
    dot_general x5 -> x0, matrix products: 16.1 us -> none  [the longest x3 12.2 us: contract(): jnp.dot(left, piece, precision=lax.Precision.HIGHEST, preferred_element_t...]
  transfers between devices with their start and end apart: 7 -> 0, of which waited for: 7 -> 0; matrix products, arithmetic and copies ran while one was open for 3% -> 0% of each run, Pallas kernels for 0% -> 0%
where the time goes in v3:
time: 80.2 us; the launch traced here: 80 us
  Pallas kernels  77.8 us (97%)
  other arithmetic  1.47 us (2%)
    pallas_call x1, Pallas kernels, grads(): pl.pallas_call(kernel, name='grads', out_shape=jax.ShapeDtypeStruct((2, 1...  77.8 us

profile of v3, /device:TPU:1, one launch (start us, length us, event | category | flops | bytes accessed | tf_op | source)
XLA Modules:
  0.0 80.0 jit_solution(13488080234465486510)
XLA Ops:
  0.6 0.0 copy-start
  0.6 0.0 copy-start.1
  0.7 0.0 copy-start.3
  0.7 0.0 copy-start.2
  0.7 0.0 copy-start.4
  0.7 0.0 copy-start.5
  0.7 77.8 %grads.1 = f32[2,16,512]{2,1,0:T(8,128)} custom-call(f32[256,128]{1,0:T(8,128)} %in_ref.1, f32[256,128]{1,0:T(8,128)} %cot_ref.1, f32[16,512]{1,0:T(8,128)} %gw_ref.1, f32[16,512]{1,0:T(8,128)} %uw_ref.1, f32[16,512]{1,0:T(8,128)} %dw_ref.1), custom_call_target="tpu_custom_call" | custom-call | tf_op jit(solution)/shard_map/grads/pallas_call | solution.py:469
  78.5 0.0 copy-done
  78.5 0.0 copy-done.1
  78.5 0.0 copy-done.3
  78.5 0.0 copy-done.2
  78.5 0.0 copy-done.4
  78.5 0.0 copy-done.5
  78.5 1.5 %divide_subtract_fusion = (f32[16,512]{1,0:T(8,128)}, f32[16,512]{1,0:T(8,128)}, f32[16,512]{1,0:T(8,128)}, f32[16,512]{1,0:T(8,128)}, f32[16,512]{1,0:T(8,128)}, /*index=5*/f32[16,512]{1,0:T(8,128)}) fusion(f32[16,512]{1,0:T(8,128)S(1)} %copy-done, f32[2,16,512]{2,1,0:T(8,128)} %grads.1, f32[16,512]{1,0:T(8,128)S(1)} %copy-done.2, ...), kind=kLoop, calls=%fused_computation.8 | loop fusion | flops 196608 | bytes 458752 | tf_op jit(solution)/shard_map/sub | solution.py:20
Async XLA Ops:
  0.6 77.9 %copy-start = (f32[16,512]{1,0:T(8,128)S(1)}, f32[16,512]{1,0:T(8,128)}, u32[]{:S(2)}) copy-start(f32[16,512]{1,0:T(8,128)} %uw_ref.1) | copy-start | bytes 98308
  0.6 77.9 %copy-start.1 = (f32[16,512]{1,0:T(8,128)S(1)}, f32[16,512]{1,0:T(8,128)}, u32[]{:S(2)}) copy-start(f32[16,512]{1,0:T(8,128)} %gw_ref.1) | copy-start | bytes 98308
  0.7 77.9 %copy-start.3 = (f32[16,512]{1,0:T(8,128)S(1)}, f32[16,512]{1,0:T(8,128)}, u32[]{:S(2)}) copy-start(f32[16,512]{1,0:T(8,128)} %param.17) | copy-start | bytes 98308
  0.7 77.9 %copy-start.2 = (f32[16,512]{1,0:T(8,128)S(1)}, f32[16,512]{1,0:T(8,128)}, u32[]{:S(2)}) copy-start(f32[16,512]{1,0:T(8,128)} %param.16) | copy-start | bytes 98308
  0.7 77.9 %copy-start.4 = (f32[16,512]{1,0:T(8,128)S(1)}, f32[16,512]{1,0:T(8,128)}, u32[]{:S(2)}) copy-start(f32[16,512]{1,0:T(8,128)} %param.15) | copy-start | bytes 98308
  0.7 77.9 %copy-start.5 = (f32[16,512]{1,0:T(8,128)S(1)}, f32[16,512]{1,0:T(8,128)}, u32[]{:S(2)}) copy-start(f32[16,512]{1,0:T(8,128)} %param.14) | copy-start | bytes 98308

commit v4 on v3

--- a/solution.py
+++ b/solution.py
@@ -38,8 +38,7 @@
     in_ref, cot_ref, gw_ref, uw_ref, dw_ref, out_ref,
     xc, w, xh, xl, ch, cl, xth, xtl, acc, rh, rl,
     gbuf, rbuf, tbuf, zbuf, gz, rz1, rz2, yz,
-    own_sem, a_recv, a_send, s_recv, s_send, o_recv, o_send, w_recv, w_send, y_recv, y_send,
-    u_recv, u_send, r_recv, r_send, z_recv, z_send, f_recv, f_send, g_recv, g_send,
+    counted, sent, own_sem, a_recv, s_recv, o_recv, w_recv, y_recv, u_recv, r_recv, z_recv, f_recv, g_recv,
 ):
     dp = lax.axis_index("dp")
     t = lax.axis_index("tensor")
@@ -78,9 +77,15 @@
         pl.semaphore_signal(barrier, inc=1, device_id=peer, device_id_type=MESH)
     pl.semaphore_wait(barrier, len(peers))
 
-    def remote(src, dst, send, recv, dev):
+    sent_rows = [0, 0, 0]
+
+    def remote(src, dst, group, recv, dev):
+        n = 1
+        for extent in src.shape:
+            n = n * extent
+        sent_rows[group] += n // 128
         pltpu.make_async_remote_copy(
-            src_ref=src, dst_ref=dst, send_sem=send, recv_sem=recv,
+            src_ref=src, dst_ref=dst, send_sem=sent.at[group], recv_sem=recv,
             device_id=dev, device_id_type=MESH,
         ).start()
 
@@ -94,17 +99,16 @@
 
     def w_own(k):
         mine = pl.ds(pl.multiple_of(c * 16, 16), 16)
-        n = k // 2
         there = pl.ds(pl.multiple_of((1 - c) * 256, 256), 256)
-        remote(w_srcs[k].at[:, there], w.at[y, k, mine, :], o_send.at[n], o_recv.at[n], sib)
+        remote(w_srcs[k].at[:, there], w.at[y, k, mine, :], 1, o_recv.at[k // 2], sib)
         here = pl.ds(pl.multiple_of(c * 256, 256), 256)
-        local_copy(w_srcs[k].at[:, here], w.at[y, k, mine, :], o_recv.at[n])
+        local_copy(w_srcs[k].at[:, here], w.at[y, k, mine, :], o_recv.at[k // 2])
 
     def w_first(k):
         for dz, dc in zpeers:
             src = w_srcs[k].at[:, pl.ds(pl.multiple_of(core_of(dc) * 256, 256), 256)]
             rows = pl.ds(pl.multiple_of((4 - dz) * 32 + c * 16, 16), 16)
-            remote(src, w.at[y, k, rows, :], w_send.at[k], w_recv.at[k], dev_of(0, dz, dc))
+            remote(src, w.at[y, k, rows, :], 1, w_recv.at[k], dev_of(0, dz, dc))
 
     U, A, B0, B1 = range(4)
 
@@ -125,7 +129,7 @@
 
     def y_start(ring, s):
         for d, r in enumerate(step_parts(ring, s, 0)):
-            remote(r, r, y_send.at[d, s - 1, ring], y_recv.at[d, s - 1, ring], ys[d])
+            remote(r, r, 1, y_recv.at[d, s - 1, ring], ys[d])
 
     def y_end(ring, s):
         for d, r in enumerate(step_parts(ring, s, 1)):
@@ -135,24 +139,24 @@
         y_end(ring, s)
         y_start(ring, s + 1)
 
-    def u_start(i):
+    def z_start(i):
         b = y_of(i)
         for d, first in enumerate((96, 32)):
             remote(
                 w.at[b, 2, pl.ds(0, 32), :], w.at[b, 2, pl.ds(first, 32), :],
-                u_send.at[0, d, i], u_recv.at[0, d, i], zs[d],
+                1, u_recv.at[0, d, i], zs[d],
             )
 
-    def u_relay(i):
+    def z_relay(i):
         b = y_of(i)
         for d, (first, src, dst) in enumerate(((96, 96, 64), (32, 48, 80))):
             wait(w.at[b, 2, pl.ds(first, 32), :], u_recv.at[0, d, i])
             remote(
                 w.at[b, 2, pl.ds(src, 16), :], w.at[b, 2, pl.ds(dst, 16), :],
-                u_send.at[1, d, i], u_recv.at[1, d, i], zs[d],
+                1, u_recv.at[1, d, i], zs[d],
             )
 
-    def u_end(i):
+    def z_end(i):
         for d in range(2):
             wait(w.at[y_of(i), 2, pl.ds(64 + 16 * d, 16), :], u_recv.at[1, d, i])
 
@@ -160,11 +164,11 @@
     rows_src = (in_ref, cot_ref)
 
     def own_to(n, j, dev, recv):
-        remote(rows_src[j], xc.at[own, c, j], a_send.at[n + j], recv, dev)
+        remote(rows_src[j], xc.at[own, c, j], 0, recv, dev)
 
     def pass_on(n, dx, dz, j, d, to_dx):
         b = xc.at[t_of(dx, dz), c, j]
-        remote(b, b, a_send.at[n], a_recv.at[to_dx, dz, j], xs[d])
+        remote(b, b, 0, a_recv.at[to_dx, dz, j], xs[d])
 
     def a_end(dx, dz, j):
         wait(xc.at[t_of(dx, dz), c, j], a_recv.at[dx, dz, j])
@@ -179,7 +183,7 @@
 
     def to_sibling(dx, dz):
         b = xc.at[t_of(dx, dz), c]
-        remote(b, b, s_send.at[dx, dz], s_recv.at[dx, dz], sib)
+        remote(b, b, 0, s_recv.at[dx, dz], sib)
 
     def s_end(dx, dz):
         wait(xc.at[t_of(dx, dz), 1 - c], s_recv.at[dx, dz])
@@ -232,21 +236,21 @@
     for j in range(2):
         own_to(4, j, zpart, a_recv.at[0, 1, j])
     for j in range(2):
-        remote(rows_src[j], xc.at[own, c, j], s_send.at[0, 0], s_recv.at[0, 0], sib)
+        remote(rows_src[j], xc.at[own, c, j], 0, s_recv.at[0, 0], sib)
         local_copy(rows_src[j], xc.at[own, c, j], own_sem)
 
     wait(part(U, y, None), o_recv.at[1])
     y_start(U, 1)
-    u_start(0)
+    z_start(0)
     wait(part(A, y, None), o_recv.at[0])
     y_start(A, 1)
     y_next(U, 1)
-    u_start(1)
-    u_start(7)
+    z_start(1)
+    z_start(7)
     y_next(A, 1)
     y_next(U, 2)
-    u_start(2)
-    u_start(6)
+    z_start(2)
+    z_start(6)
     from_left(0)
     wait(part(B0, y, None), w_recv.at[0])
     y_start(B0, 1)
@@ -257,8 +261,8 @@
     to_sibling(3, 0)
     y_next(A, 2)
     y_next(U, 3)
-    u_start(3)
-    u_start(5)
+    z_start(3)
+    z_start(5)
     wait(part(B1, y, None), w_recv.at[1])
     y_start(B1, 1)
     a_end(0, 1, 0)
@@ -270,20 +274,21 @@
     to_sibling(2, 0)
     y_next(A, 3)
     y_end(U, 4)
-    u_start(4)
+    z_start(4)
+    y_next(B1, 1)
     a_end(0, 1, 1)
     pass_on(9, 0, 1, 1, 1, 1)
     pass_on(7, 0, 1, 1, 0, 3)
     to_sibling(0, 1)
+    y_next(B0, 2)
     wait(xc.at[own, c], own_sem)
     s_end(0, 0)
     s_end(1, 0)
     s_end(3, 0)
     convert_many(6, lambda i: (lax.rem(x + 3 + i // 2, NX) * NZL + zl, lax.rem(i, 2)))
     from_left(1)
-    y_next(B1, 1)
-    u_relay(0)
-    y_next(B0, 2)
+    z_relay(0)
+    y_next(B1, 2)
     s_end(2, 0)
     convert_many(2, lambda i: (lax.rem(x + 2, NX) * NZL + zl, i))
     s_end(0, 1)
@@ -293,142 +298,146 @@
     to_sibling(1, 1)
     a_end(3, 1, 1)
     to_sibling(3, 1)
-    u_relay(1)
-    u_relay(7)
-    y_next(B1, 2)
-    u_relay(2)
-    u_relay(6)
     y_next(B0, 3)
+    z_relay(1)
+    z_relay(7)
+    z_relay(2)
+    z_relay(6)
+    for j in range(2):
+        a_end(2, 1, j)
+    to_sibling(2, 1)
+    y_next(B1, 3)
     s_end(1, 1)
     s_end(3, 1)
     convert_many(4, lambda i: (lax.rem(x + 3 + 2 * (i // 2), NX) * NZL + 1 - zl, lax.rem(i, 2)))
-    for j in range(2):
-        a_end(2, 1, j)
-    to_sibling(2, 1)
-    u_relay(3)
-    u_relay(5)
-    y_next(B1, 3)
-    u_relay(4)
+    z_relay(3)
+    z_relay(5)
+    z_relay(4)
     s_end(2, 1)
     convert_many(2, lambda i: (lax.rem(x + 2, NX) * NZL + 1 - zl, i))
     pairs = [(y_of(d), y_of(8 - d)) for d in range(1, 4)] + [(y, y_of(4))]
     for k in range(2):
         for i in range(3):
             forward(pairs[i], k, i == 0)
-    for i in range(3):
-        u_end(i + 1)
-        u_end(7 - i)
-        forward(pairs[i], 2, i == 0)
     y_end(A, 4)
     y_end(B0, 4)
-    forward(pairs[3], 0)
     y_end(B1, 4)
-    forward(pairs[3], 1)
-    u_end(0)
-    u_end(4)
-    forward(pairs[3], 2)
-
-    def rows_body(r, carry):
-        rows = pl.ds(pl.multiple_of(r * 64, 64), 64)
-        back = acc[0, rows, :]
-        gate = acc[1, rows, :]
-        lift = acc[2, rows, :]
-        s = 1.0 / (1.0 + jnp.exp(-gate))
-        bs = back * s
-        hi, lo = split(bs * lift * (1.0 + gate * (1.0 - s)))
-        rh[rows, 0:256] = hi
-        rl[rows, 0:256] = lo
-        hi, lo = split(bs * gate)
-        rh[rows, 256:512] = hi
-        rl[rows, 256:512] = lo
-        return carry
-
-    lax.fori_loop(0, 8, rows_body, 0)
-
-    def backward(bs):
-        h = jnp.concatenate([xth[b] for b in bs], axis=0) if len(bs) == 2 else xth[bs[0]]
-        l = jnp.concatenate([xtl[b] for b in bs], axis=0) if len(bs) == 2 else xtl[bs[0]]
-        v = dot3(h, l, rh[:, 0:384], rl[:, 0:384])
+    for k in range(2):
+        forward(pairs[3], k)
+
+    def grad_rows(m):
+        def body(r, carry):
+            rows = pl.ds(pl.multiple_of(r * 64, 64), 64)
+            gate = acc[1, rows, :]
+            s = 1.0 / (1.0 + jnp.exp(-gate))
+            bs = acc[0, rows, :] * s
+            v = bs * gate if m == 1 else bs * acc[2, rows, :] * (1.0 + gate * (1.0 - s))
+            hi, lo = split(v)
+            rh[m, rows, :] = hi
+            rl[m, rows, :] = lo
+            return carry
+
+        lax.fori_loop(0, 8, body, 0)
+
+    def backward(bs, m):
+        h = jnp.concatenate([xth[b] for b in bs], axis=0)
+        l = jnp.concatenate([xtl[b] for b in bs], axis=0)
+        v = dot3(h, l, rh[m], rl[m])
         for i, b in enumerate(bs):
-            for q in range(3):
-                gbuf[b, q] = v[i * 128 : (i + 1) * 128, q * 128 : (q + 1) * 128]
-
-    def backward_last(i, carry):
-        h = jnp.concatenate([xth[2 * i], xth[2 * i + 1]], axis=0)
-        l = jnp.concatenate([xtl[2 * i], xtl[2 * i + 1]], axis=0)
-        v = dot3(h, l, rh[:, 384:512], rl[:, 384:512])
-        gz[2 * i] = v[0:128]
-        gz[2 * i + 1] = v[128:256]
-        return carry
+            rows = slice(i * 128, i * 128 + 128)
+            gbuf[b, 2 * m] = v[rows, 0:128]
+            if m == 0:
+                gbuf[b, 1] = v[rows, 128:256]
+            else:
+                gz[b] = v[rows, 128:256]
 
     def r_start(s, q, d):
         b = y_of(5 - s) if d == 0 else y_of(3 + s)
         rows = pl.ds(64 * d, 64) if s == 1 else pl.ds(0, 128)
         remote(
             gbuf.at[b, q, rows, :], rbuf.at[d, s - 1, q, rows, :],
-            r_send.at[d, s - 1, q], r_recv.at[d, s - 1, q], ys[d],
+            2, r_recv.at[d, s - 1, q], ys[d],
         )
 
-    def r_step(s):
-        for q in range(3):
+    def r_step(s, *qs):
+        for q in qs:
             for d in range(2):
+                if s == 1:
+                    r_start(s, q, d)
+                    continue
                 b = y_of(5 - s) if d == 0 else y_of(3 + s)
                 rows = pl.ds(64 * d, 64) if s == 2 else pl.ds(0, 128)
                 wait(rbuf.at[d, s - 2, q, rows, :], r_recv.at[d, s - 2, q])
                 gbuf[b, q, rows, :] += rbuf[d, s - 2, q, rows, :]
                 r_start(s, q, d)
 
+    def r_end(q):
+        for d in range(2):
+            wait(rbuf.at[d, 3, q], r_recv.at[d, 3, q])
+        for i in range(8):
+            rows = pl.ds(16 * i, 16)
+            tbuf[q, i] = gbuf[y, q, rows, :] + rbuf[0, 3, q, rows, :] + rbuf[1, 3, q, rows, :]
+        src = zh * 2 + c
+        for dz, dc in zpeers + [(0, 1)]:
+            remote(
+                tbuf.at[q, zat[dz] * 2 + core_of(dc)], zbuf.at[q, src],
+                2, z_recv.at[q], dev_of(0, dz, dc),
+            )
+        zbuf[q, src] = tbuf[q, src]
+
     def z_rows(d, first, n):
         return pl.ds(pl.multiple_of(zat[d] * 32 + first, 16), n)
 
-    backward((y_of(4),))
-    for q in range(3):
-        for d in range(2):
-            r_start(1, q, d)
-    lax.fori_loop(0, 4, backward_last, 0)
+    grad_rows(1)
+    backward(pairs[3], 1)
+    r_step(1, 2)
+    for i in range(3):
+        z_end(i + 1)
+        z_end(7 - i)
+    for i in range(3):
+        forward(pairs[i], 2, i == 0)
+    z_end(0)
+    z_end(4)
+    forward(pairs[3], 2)
+    grad_rows(0)
+    backward(pairs[3], 0)
+    r_step(1, 0, 1)
+    for i in (2, 1, 0):
+        backward(pairs[i], 1)
     for d in range(2):
-        remote(gz.at[:, z_rows(2, 16 * d, 16), :], rz1.at[d], f_send.at[0, d], f_recv.at[0, d], zs[d])
-    backward((y_of(3), y_of(5)))
-    r_step(2)
-    backward((y_of(2), y_of(6)))
+        remote(gz.at[:, z_rows(2, 16 * d, 16), :], rz1.at[d], 2, f_recv.at[0, d], zs[d])
+    r_step(2, 2)
+    backward(pairs[2], 0)
+    r_step(2, 0, 1)
+    r_step(3, 2)
     for d, dz in ((0, 1), (1, 3)):
         wait(rz1.at[d], f_recv.at[0, d])
         rows = z_rows(dz, 16 * d, 16)
         gz[:, rows, :] = gz[:, rows, :] + rz1[d]
-        remote(gz.at[:, z_rows(dz, 0, 32), :], rz2.at[d], f_send.at[1, d], f_recv.at[1, d], zs[d])
-    r_step(3)
-    backward((y_of(1), y_of(7)))
-    r_step(4)
-    backward((y,))
+        remote(gz.at[:, z_rows(dz, 0, 32), :], rz2.at[d], 2, f_recv.at[1, d], zs[d])
+    backward(pairs[1], 0)
+    r_step(3, 0, 1)
+    backward(pairs[0], 0)
+    r_step(4, 2)
+    r_step(4, 0, 1)
+    r_end(2)
     for d in range(2):
         wait(rz2.at[d], f_recv.at[1, d])
     rows = z_rows(0, 0, 32)
     gz[:, rows, :] = gz[:, rows, :] + rz2[0] + rz2[1]
     for dy, dc in ypeers + [(0, 1)]:
         rows = pl.ds(pl.multiple_of(zh * 32 + core_of(dc) * 16, 16), 16)
-        remote(gz.at[y_of(dy), rows, :], yz.at[y * 2 + c], g_send, g_recv, dev_of(dy, 0, dc))
+        remote(gz.at[y_of(dy), rows, :], yz.at[y * 2 + c], 2, g_recv, dev_of(dy, 0, dc))
     yz[y * 2 + c] = gz[y, pl.ds(pl.multiple_of(zh * 32 + c * 16, 16), 16), :]
-
-    src = zh * 2 + c
-    for q in range(3):
-        for d in range(2):
-            wait(rbuf.at[d, 3, q], r_recv.at[d, 3, q])
-        for i in range(8):
-            rows = pl.ds(16 * i, 16)
-            tbuf[q, i] = gbuf[y, q, rows, :] + rbuf[0, 3, q, rows, :] + rbuf[1, 3, q, rows, :]
-        for dz, dc in zpeers + [(0, 1)]:
-            remote(
-                tbuf.at[q, zat[dz] * 2 + core_of(dc)], zbuf.at[q, src],
-                z_send.at[q], z_recv.at[q], dev_of(0, dz, dc),
-            )
-        zbuf[q, src] = tbuf[q, src]
+    r_end(0)
+    r_end(1)
     wait(yz.at[pl.ds(0, 15)], g_recv)
     for cc in range(2):
         v = yz[cc]
         for i in range(1, NY):
             v = v + yz[2 * i + cc]
         out_ref[1, :, cc * 256 + 128 : cc * 256 + 256] = v
-    for q in range(3):
+    for q in (2, 0, 1):
         wait(zbuf.at[q, pl.ds(0, 7)], z_recv.at[q])
         for cc in range(2):
             col = cc * 256 + (q % 2) * 128
@@ -436,32 +445,8 @@
                 (zbuf[q, cc] + zbuf[q, 2 + cc]) + (zbuf[q, 4 + cc] + zbuf[q, 6 + cc])
             )
 
-    def sent(rows, sem):
-        wait(w.at[0, 0, pl.ds(0, rows), :], sem)
-
-    sent(32, o_send.at[0])
-    sent(16, o_send.at[1])
-    sent(96, w_send.at[0])
-    sent(96, w_send.at[1])
-    for n in range(14):
-        sent(128, a_send.at[n])
-    for dx in range(4):
-        for dz in range(2):
-            wait(xc.at[0, 0], s_send.at[dx, dz])
-    for d in range(2):
-        for s in range(4):
-            for ring, rows in ((U, 32), (A, 64), (B0, 96), (B1, 96)):
-                sent(rows // 2 if s == 3 else rows, y_send.at[d, s, ring])
-            for q in range(3):
-                sent(32 if s == 0 else 64, r_send.at[d, s, q])
-        for i in range(NY):
-            sent(32, u_send.at[0, d, i])
-            sent(16, u_send.at[1, d, i])
-        sent(64, f_send.at[0, d])
-        sent(128, f_send.at[1, d])
-    for q in range(3):
-        sent(56, z_send.at[q])
-    sent(120, g_send)
+    for group in range(3):
+        wait(counted.at[pl.ds(0, sent_rows[group]), :], sent.at[group])
 
 
 def grads(inputs, cotangent, gate_weight, up_weight, down_weight):
@@ -482,8 +467,8 @@
             pltpu.VMEM((8, 128, 512), BF16),
             pltpu.VMEM((8, 128, 512), BF16),
             pltpu.VMEM((3, 512, 256), F32),
-            pltpu.VMEM((512, 512), BF16),
-            pltpu.VMEM((512, 512), BF16),
+            pltpu.VMEM((2, 512, 256), BF16),
+            pltpu.VMEM((2, 512, 256), BF16),
             pltpu.VMEM((8, 3, 128, 128), F32),
             pltpu.VMEM((2, 4, 3, 128, 128), F32),
             pltpu.VMEM((3, 8, 16, 128), F32),
@@ -492,26 +477,18 @@
             pltpu.VMEM((2, 8, 16, 128), F32),
             pltpu.VMEM((2, 8, 32, 128), F32),
             pltpu.VMEM((16, 16, 128), F32),
+            pltpu.VMEM((8192, 128), F32),
+            dma((3,)),
             dma,
             dma((4, 2, 2)),
-            dma((14,)),
-            dma((4, 2)),
             dma((4, 2)),
             dma((2,)),
             dma((2,)),
-            dma((2,)),
-            dma((2,)),
-            dma((2, 4, 4)),
             dma((2, 4, 4)),
             dma((2, 2, 8)),
-            dma((2, 2, 8)),
-            dma((2, 4, 3)),
             dma((2, 4, 3)),
             dma((3,)),
-            dma((3,)),
             dma((2, 2)),
-            dma((2, 2)),
-            dma,
             dma,
         ],
         compiler_params=pltpu.CompilerParams(

time: 80.2 us -> 77.1 us (0.961)
  Pallas kernels: 77.8 us -> 74.6 us
    pallas_call x1, Pallas kernels: 77.8 us -> 74.6 us  [grads(): pl.pallas_call(kernel, name='grads', out_shape=jax.ShapeDtypeStruct((2, 1...]
where the time goes in v4:
time: 77.1 us; the launch traced here: 76.8 us
  Pallas kernels  74.6 us (97%)
  other arithmetic  1.47 us (2%)
    pallas_call x1, Pallas kernels, grads(): pl.pallas_call(kernel, name='grads', out_shape=jax.ShapeDtypeStruct((2, 1...  74.6 us

profile of v4, /device:TPU:1, one launch (start us, length us, event | category | flops | bytes accessed | tf_op | source)
XLA Modules:
  0.0 76.8 jit_solution(6156160269098346547)
XLA Ops:
  0.6 0.0 copy-start
  0.6 0.0 copy-start.1
  0.7 0.0 copy-start.3
  0.7 0.0 copy-start.2
  0.7 0.0 copy-start.4
  0.7 0.0 copy-start.5
  0.7 74.6 %grads.1 = f32[2,16,512]{2,1,0:T(8,128)} custom-call(f32[256,128]{1,0:T(8,128)} %in_ref.1, f32[256,128]{1,0:T(8,128)} %cot_ref.1, f32[16,512]{1,0:T(8,128)} %gw_ref.1, f32[16,512]{1,0:T(8,128)} %uw_ref.1, f32[16,512]{1,0:T(8,128)} %dw_ref.1), custom_call_target="tpu_custom_call" | custom-call | tf_op jit(solution)/shard_map/grads/pallas_call | solution.py:454
  75.3 0.0 copy-done
  75.3 0.0 copy-done.1
  75.3 0.0 copy-done.3
  75.4 0.0 copy-done.2
  75.4 0.0 copy-done.4
  75.4 0.0 copy-done.5
  75.4 1.5 %divide_subtract_fusion = (f32[16,512]{1,0:T(8,128)}, f32[16,512]{1,0:T(8,128)}, f32[16,512]{1,0:T(8,128)}, f32[16,512]{1,0:T(8,128)}, f32[16,512]{1,0:T(8,128)}, /*index=5*/f32[16,512]{1,0:T(8,128)}) fusion(f32[16,512]{1,0:T(8,128)S(1)} %copy-done, f32[2,16,512]{2,1,0:T(8,128)} %grads.1, f32[16,512]{1,0:T(8,128)S(1)} %copy-done.2, ...), kind=kLoop, calls=%fused_computation.8 | loop fusion | flops 196608 | bytes 458752 | tf_op jit(solution)/shard_map/sub | solution.py:20
Async XLA Ops:
  0.6 74.7 %copy-start = (f32[16,512]{1,0:T(8,128)S(1)}, f32[16,512]{1,0:T(8,128)}, u32[]{:S(2)}) copy-start(f32[16,512]{1,0:T(8,128)} %uw_ref.1) | copy-start | bytes 98308
  0.6 74.7 %copy-start.1 = (f32[16,512]{1,0:T(8,128)S(1)}, f32[16,512]{1,0:T(8,128)}, u32[]{:S(2)}) copy-start(f32[16,512]{1,0:T(8,128)} %gw_ref.1) | copy-start | bytes 98308
  0.7 74.7 %copy-start.3 = (f32[16,512]{1,0:T(8,128)S(1)}, f32[16,512]{1,0:T(8,128)}, u32[]{:S(2)}) copy-start(f32[16,512]{1,0:T(8,128)} %param.17) | copy-start | bytes 98308
  0.7 74.7 %copy-start.2 = (f32[16,512]{1,0:T(8,128)S(1)}, f32[16,512]{1,0:T(8,128)}, u32[]{:S(2)}) copy-start(f32[16,512]{1,0:T(8,128)} %param.16) | copy-start | bytes 98308
  0.7 74.7 %copy-start.4 = (f32[16,512]{1,0:T(8,128)S(1)}, f32[16,512]{1,0:T(8,128)}, u32[]{:S(2)}) copy-start(f32[16,512]{1,0:T(8,128)} %param.15) | copy-start | bytes 98308
  0.7 74.7 %copy-start.5 = (f32[16,512]{1,0:T(8,128)S(1)}, f32[16,512]{1,0:T(8,128)}, u32[]{:S(2)}) copy-start(f32[16,512]{1,0:T(8,128)} %param.14) | copy-start | bytes 98308

commit v5 on v4

--- a/solution.py
+++ b/solution.py
@@ -95,6 +95,9 @@
     def wait(ref, sem):
         pltpu.make_async_copy(ref, ref, sem).wait()
 
+    def wait_rows(n, sem):
+        wait(counted.at[pl.ds(0, n), :], sem)
+
     w_srcs = (dw_ref, gw_ref, uw_ref)
 
     def w_own(k):
@@ -129,11 +132,10 @@
 
     def y_start(ring, s):
         for d, r in enumerate(step_parts(ring, s, 0)):
-            remote(r, r, 1, y_recv.at[d, s - 1, ring], ys[d])
+            remote(r, r, 1, y_recv.at[s - 1, ring], ys[d])
 
     def y_end(ring, s):
-        for d, r in enumerate(step_parts(ring, s, 1)):
-            wait(r, y_recv.at[d, s - 1, ring])
+        wait_rows((128, 256, 384, 384)[ring] // (2 if s == 4 else 1), y_recv.at[s - 1, ring])
 
     def y_next(ring, s):
         y_end(ring, s)
@@ -142,23 +144,16 @@
     def z_start(i):
         b = y_of(i)
         for d, first in enumerate((96, 32)):
-            remote(
-                w.at[b, 2, pl.ds(0, 32), :], w.at[b, 2, pl.ds(first, 32), :],
-                1, u_recv.at[0, d, i], zs[d],
-            )
+            remote(w.at[b, 2, pl.ds(0, 32), :], w.at[b, 2, pl.ds(first, 32), :], 1, u_recv.at[0, i], zs[d])
 
     def z_relay(i):
         b = y_of(i)
-        for d, (first, src, dst) in enumerate(((96, 96, 64), (32, 48, 80))):
-            wait(w.at[b, 2, pl.ds(first, 32), :], u_recv.at[0, d, i])
-            remote(
-                w.at[b, 2, pl.ds(src, 16), :], w.at[b, 2, pl.ds(dst, 16), :],
-                1, u_recv.at[1, d, i], zs[d],
-            )
+        wait_rows(128, u_recv.at[0, i])
+        for d, (src, dst) in enumerate(((96, 64), (48, 80))):
+            remote(w.at[b, 2, pl.ds(src, 16), :], w.at[b, 2, pl.ds(dst, 16), :], 1, u_recv.at[1, i], zs[d])
 
     def z_end(i):
-        for d in range(2):
-            wait(w.at[y_of(i), 2, pl.ds(64 + 16 * d, 16), :], u_recv.at[1, d, i])
+        wait_rows(64, u_recv.at[1, i])
 
     own = t_of(0, 0)
     rows_src = (in_ref, cot_ref)
@@ -265,10 +260,10 @@
     z_start(5)
     wait(part(B1, y, None), w_recv.at[1])
     y_start(B1, 1)
+    y_next(B0, 1)
     a_end(0, 1, 0)
     pass_on(6, 0, 1, 0, 0, 3)
     pass_on(8, 0, 1, 0, 1, 1)
-    y_next(B0, 1)
     for j in range(2):
         a_end(2, 0, j)
     to_sibling(2, 0)
@@ -288,6 +283,8 @@
     convert_many(6, lambda i: (lax.rem(x + 3 + i // 2, NX) * NZL + zl, lax.rem(i, 2)))
     from_left(1)
     z_relay(0)
+    z_relay(1)
+    z_relay(7)
     y_next(B1, 2)
     s_end(2, 0)
     convert_many(2, lambda i: (lax.rem(x + 2, NX) * NZL + zl, i))
@@ -299,20 +296,18 @@
     a_end(3, 1, 1)
     to_sibling(3, 1)
     y_next(B0, 3)
-    z_relay(1)
-    z_relay(7)
     z_relay(2)
     z_relay(6)
-    for j in range(2):
-        a_end(2, 1, j)
+    z_relay(3)
+    z_relay(5)
+    a_end(2, 1, 0)
+    y_next(B1, 3)
+    a_end(2, 1, 1)
     to_sibling(2, 1)
-    y_next(B1, 3)
+    z_relay(4)
     s_end(1, 1)
     s_end(3, 1)
     convert_many(4, lambda i: (lax.rem(x + 3 + 2 * (i // 2), NX) * NZL + 1 - zl, lax.rem(i, 2)))
-    z_relay(3)
-    z_relay(5)
-    z_relay(4)
     s_end(2, 1)
     convert_many(2, lambda i: (lax.rem(x + 2, NX) * NZL + 1 - zl, i))
     pairs = [(y_of(d), y_of(8 - d)) for d in range(1, 4)] + [(y, y_of(4))]
@@ -340,8 +335,8 @@
         lax.fori_loop(0, 8, body, 0)
 
     def backward(bs, m):
-        h = jnp.concatenate([xth[b] for b in bs], axis=0)
-        l = jnp.concatenate([xtl[b] for b in bs], axis=0)
+        h = jnp.concatenate([xth[b] for b in bs], axis=0) if len(bs) == 2 else xth[bs[0]]
+        l = jnp.concatenate([xtl[b] for b in bs], axis=0) if len(bs) == 2 else xtl[bs[0]]
         v = dot3(h, l, rh[m], rl[m])
         for i, b in enumerate(bs):
             rows = slice(i * 128, i * 128 + 128)
@@ -356,24 +351,22 @@
         rows = pl.ds(64 * d, 64) if s == 1 else pl.ds(0, 128)
         remote(
             gbuf.at[b, q, rows, :], rbuf.at[d, s - 1, q, rows, :],
-            2, r_recv.at[d, s - 1, q], ys[d],
+            2, r_recv.at[s - 1, q], ys[d],
         )
 
     def r_step(s, *qs):
         for q in qs:
+            if s > 1:
+                wait_rows(128 if s == 2 else 256, r_recv.at[s - 2, q])
             for d in range(2):
-                if s == 1:
-                    r_start(s, q, d)
-                    continue
                 b = y_of(5 - s) if d == 0 else y_of(3 + s)
                 rows = pl.ds(64 * d, 64) if s == 2 else pl.ds(0, 128)
-                wait(rbuf.at[d, s - 2, q, rows, :], r_recv.at[d, s - 2, q])
-                gbuf[b, q, rows, :] += rbuf[d, s - 2, q, rows, :]
+                if s > 1:
+                    gbuf[b, q, rows, :] += rbuf[d, s - 2, q, rows, :]
                 r_start(s, q, d)
 
     def r_end(q):
-        for d in range(2):
-            wait(rbuf.at[d, 3, q], r_recv.at[d, 3, q])
+        wait_rows(256, r_recv.at[3, q])
         for i in range(8):
             rows = pl.ds(16 * i, 16)
             tbuf[q, i] = gbuf[y, q, rows, :] + rbuf[0, 3, q, rows, :] + rbuf[1, 3, q, rows, :]
@@ -389,7 +382,7 @@
         return pl.ds(pl.multiple_of(zat[d] * 32 + first, 16), n)
 
     grad_rows(1)
-    backward(pairs[3], 1)
+    backward((y_of(4),), 1)
     r_step(1, 2)
     for i in range(3):
         z_end(i + 1)
@@ -400,10 +393,11 @@
     z_end(4)
     forward(pairs[3], 2)
     grad_rows(0)
-    backward(pairs[3], 0)
+    backward((y_of(4),), 0)
     r_step(1, 0, 1)
     for i in (2, 1, 0):
         backward(pairs[i], 1)
+    backward((y,), 1)
     for d in range(2):
         remote(gz.at[:, z_rows(2, 16 * d, 16), :], rz1.at[d], 2, f_recv.at[0, d], zs[d])
     r_step(2, 2)
@@ -420,6 +414,7 @@
     backward(pairs[0], 0)
     r_step(4, 2)
     r_step(4, 0, 1)
+    backward((y,), 0)
     r_end(2)
     for d in range(2):
         wait(rz2.at[d], f_recv.at[1, d])
@@ -484,9 +479,9 @@
             dma((4, 2)),
             dma((2,)),
             dma((2,)),
-            dma((2, 4, 4)),
-            dma((2, 2, 8)),
-            dma((2, 4, 3)),
+            dma((4, 4)),
+            dma((2, 8)),
+            dma((4, 3)),
             dma((3,)),
             dma((2, 2)),
             dma,

time: 77.1 us -> 76.6 us (level)
  no operation moved by 1% of the time
where the time goes in v5:
time: 76.6 us; the launch traced here: 76.3 us
  Pallas kernels  74.1 us (97%)
  other arithmetic  1.47 us (2%)
    pallas_call x1, Pallas kernels, grads(): pl.pallas_call(kernel, name='grads', out_shape=jax.ShapeDtypeStruct((2, 1...  74.1 us

profile of v5, /device:TPU:1, one launch (start us, length us, event | category | flops | bytes accessed | tf_op | source)
XLA Modules:
  0.0 76.3 jit_solution(16512671462549384357)
XLA Ops:
  0.6 0.0 copy-start
  0.6 0.0 copy-start.1
  0.7 0.0 copy-start.3
  0.7 0.0 copy-start.2
  0.7 0.0 copy-start.4
  0.7 0.0 copy-start.5
  0.7 74.1 %grads.1 = f32[2,16,512]{2,1,0:T(8,128)} custom-call(f32[256,128]{1,0:T(8,128)} %in_ref.1, f32[256,128]{1,0:T(8,128)} %cot_ref.1, f32[16,512]{1,0:T(8,128)} %gw_ref.1, f32[16,512]{1,0:T(8,128)} %uw_ref.1, f32[16,512]{1,0:T(8,128)} %dw_ref.1), custom_call_target="tpu_custom_call" | custom-call | tf_op jit(solution)/shard_map/grads/pallas_call | solution.py:449
  74.8 0.0 copy-done
  74.8 0.0 copy-done.1
  74.8 0.0 copy-done.3
  74.8 0.0 copy-done.2
  74.8 0.0 copy-done.4
  74.8 0.0 copy-done.5
  74.9 1.5 %divide_subtract_fusion = (f32[16,512]{1,0:T(8,128)}, f32[16,512]{1,0:T(8,128)}, f32[16,512]{1,0:T(8,128)}, f32[16,512]{1,0:T(8,128)}, f32[16,512]{1,0:T(8,128)}, /*index=5*/f32[16,512]{1,0:T(8,128)}) fusion(f32[16,512]{1,0:T(8,128)S(1)} %copy-done, f32[2,16,512]{2,1,0:T(8,128)} %grads.1, f32[16,512]{1,0:T(8,128)S(1)} %copy-done.2, ...), kind=kLoop, calls=%fused_computation.8 | loop fusion | flops 196608 | bytes 458752 | tf_op jit(solution)/shard_map/sub | solution.py:20
Async XLA Ops:
  0.6 74.2 %copy-start = (f32[16,512]{1,0:T(8,128)S(1)}, f32[16,512]{1,0:T(8,128)}, u32[]{:S(2)}) copy-start(f32[16,512]{1,0:T(8,128)} %uw_ref.1) | copy-start | bytes 98308
  0.6 74.2 %copy-start.1 = (f32[16,512]{1,0:T(8,128)S(1)}, f32[16,512]{1,0:T(8,128)}, u32[]{:S(2)}) copy-start(f32[16,512]{1,0:T(8,128)} %gw_ref.1) | copy-start | bytes 98308
  0.7 74.2 %copy-start.3 = (f32[16,512]{1,0:T(8,128)S(1)}, f32[16,512]{1,0:T(8,128)}, u32[]{:S(2)}) copy-start(f32[16,512]{1,0:T(8,128)} %param.17) | copy-start | bytes 98308
  0.7 74.2 %copy-start.2 = (f32[16,512]{1,0:T(8,128)S(1)}, f32[16,512]{1,0:T(8,128)}, u32[]{:S(2)}) copy-start(f32[16,512]{1,0:T(8,128)} %param.16) | copy-start | bytes 98308
  0.7 74.2 %copy-start.4 = (f32[16,512]{1,0:T(8,128)S(1)}, f32[16,512]{1,0:T(8,128)}, u32[]{:S(2)}) copy-start(f32[16,512]{1,0:T(8,128)} %param.15) | copy-start | bytes 98308
  0.7 74.2 %copy-start.5 = (f32[16,512]{1,0:T(8,128)S(1)}, f32[16,512]{1,0:T(8,128)}, u32[]{:S(2)}) copy-start(f32[16,512]{1,0:T(8,128)} %param.14) | copy-start | bytes 98308

commit v6 on v5

--- a/solution.py
+++ b/solution.py
@@ -236,16 +236,11 @@
 
     wait(part(U, y, None), o_recv.at[1])
     y_start(U, 1)
-    z_start(0)
     wait(part(A, y, None), o_recv.at[0])
     y_start(A, 1)
     y_next(U, 1)
-    z_start(1)
-    z_start(7)
     y_next(A, 1)
     y_next(U, 2)
-    z_start(2)
-    z_start(6)
     from_left(0)
     wait(part(B0, y, None), w_recv.at[0])
     y_start(B0, 1)
@@ -256,10 +251,10 @@
     to_sibling(3, 0)
     y_next(A, 2)
     y_next(U, 3)
-    z_start(3)
-    z_start(5)
     wait(part(B1, y, None), w_recv.at[1])
     y_start(B1, 1)
+    for i in (0, 1, 7, 2, 6, 3, 5):
+        z_start(i)
     y_next(B0, 1)
     a_end(0, 1, 0)
     pass_on(6, 0, 1, 0, 0, 3)

time: 76.6 us -> 76.7 us (level)
  no operation moved by 1% of the time
where the time goes in v6:
time: 76.7 us; the launch traced here: 76.5 us
  Pallas kernels  74.2 us (97%)
  other arithmetic  1.47 us (2%)
    pallas_call x1, Pallas kernels, grads(): pl.pallas_call(kernel, name='grads', out_shape=jax.ShapeDtypeStruct((2, 1...  74.2 us

profile of v6, /device:TPU:1, one launch (start us, length us, event | category | flops | bytes accessed | tf_op | source)
XLA Modules:
  0.0 76.5 jit_solution(4220839106745473973)
XLA Ops:
  0.6 0.0 copy-start
  0.6 0.0 copy-start.1
  0.7 0.0 copy-start.3
  0.7 0.0 copy-start.2
  0.7 0.0 copy-start.4
  0.7 0.0 copy-start.5
  0.7 74.2 %grads.1 = f32[2,16,512]{2,1,0:T(8,128)} custom-call(f32[256,128]{1,0:T(8,128)} %in_ref.1, f32[256,128]{1,0:T(8,128)} %cot_ref.1, f32[16,512]{1,0:T(8,128)} %gw_ref.1, f32[16,512]{1,0:T(8,128)} %uw_ref.1, f32[16,512]{1,0:T(8,128)} %dw_ref.1), custom_call_target="tpu_custom_call" | custom-call | tf_op jit(solution)/shard_map/grads/pallas_call | solution.py:444
  74.9 0.0 copy-done
  74.9 0.0 copy-done.1
  75.0 0.0 copy-done.3
  75.0 0.0 copy-done.2
  75.0 0.0 copy-done.4
  75.0 0.0 copy-done.5
  75.0 1.5 %divide_subtract_fusion = (f32[16,512]{1,0:T(8,128)}, f32[16,512]{1,0:T(8,128)}, f32[16,512]{1,0:T(8,128)}, f32[16,512]{1,0:T(8,128)}, f32[16,512]{1,0:T(8,128)}, /*index=5*/f32[16,512]{1,0:T(8,128)}) fusion(f32[16,512]{1,0:T(8,128)S(1)} %copy-done, f32[2,16,512]{2,1,0:T(8,128)} %grads.1, f32[16,512]{1,0:T(8,128)S(1)} %copy-done.2, ...), kind=kLoop, calls=%fused_computation.8 | loop fusion | flops 196608 | bytes 458752 | tf_op jit(solution)/shard_map/sub | solution.py:20
Async XLA Ops:
  0.6 74.3 %copy-start = (f32[16,512]{1,0:T(8,128)S(1)}, f32[16,512]{1,0:T(8,128)}, u32[]{:S(2)}) copy-start(f32[16,512]{1,0:T(8,128)} %uw_ref.1) | copy-start | bytes 98308
  0.6 74.3 %copy-start.1 = (f32[16,512]{1,0:T(8,128)S(1)}, f32[16,512]{1,0:T(8,128)}, u32[]{:S(2)}) copy-start(f32[16,512]{1,0:T(8,128)} %gw_ref.1) | copy-start | bytes 98308
  0.7 74.3 %copy-start.3 = (f32[16,512]{1,0:T(8,128)S(1)}, f32[16,512]{1,0:T(8,128)}, u32[]{:S(2)}) copy-start(f32[16,512]{1,0:T(8,128)} %param.17) | copy-start | bytes 98308
  0.7 74.3 %copy-start.2 = (f32[16,512]{1,0:T(8,128)S(1)}, f32[16,512]{1,0:T(8,128)}, u32[]{:S(2)}) copy-start(f32[16,512]{1,0:T(8,128)} %param.16) | copy-start | bytes 98308
  0.7 74.3 %copy-start.4 = (f32[16,512]{1,0:T(8,128)S(1)}, f32[16,512]{1,0:T(8,128)}, u32[]{:S(2)}) copy-start(f32[16,512]{1,0:T(8,128)} %param.15) | copy-start | bytes 98308
  0.7 74.3 %copy-start.5 = (f32[16,512]{1,0:T(8,128)S(1)}, f32[16,512]{1,0:T(8,128)}, u32[]{:S(2)}) copy-start(f32[16,512]{1,0:T(8,128)} %param.14) | copy-start | bytes 98308
